TPU v7x, 32 devices: a whole 2x2x4 slice. The times are simulated.
32 devices in a mesh: dp: 16 (over z, x, core), tensor: 2 (over y).
Axes of the slice: x: 2, y: 2, z: 4, core: 2. Of those that a mesh axis runs over, the one named last changes fastest.
Arguments:
- tokens: bfloat16 [16384, 1024], P(('dp', 'tensor')), may hold values from -6 to 6
- cotangent: bfloat16 [16384, 1024], P(('dp', 'tensor')), may hold values from -6 to 6
- lengths: int32 [16, 8], P('dp'), may hold values from 1 to 512, 1024 in all within a row
- ln1_gain: bfloat16 [1024], P('dp'), may hold values from 0.5 to 1.5
- ln1_bias: bfloat16 [1024], P('dp'), may hold values from -3 to 3
- qkv_weight: bfloat16 [1024, 3, 1024], P('dp', None, 'tensor')
- qkv_bias: bfloat16 [2, 16, 64], P(None, 'tensor', 'dp'), may hold values from -3 to 3
- out_weight: bfloat16 [1024, 1024], P('tensor', 'dp'), may hold values from -0.375 to 0.375
- out_bias: bfloat16 [1024], P('dp'), may hold values from -3 to 3
- ln2_gain: bfloat16 [1024], P('dp'), may hold values from 0.5 to 1.5
- ln2_bias: bfloat16 [1024], P('dp'), may hold values from -3 to 3
- up_weight: bfloat16 [1024, 4096], P('dp', 'tensor'), may hold values from -0.1875 to 0.1875
- up_bias: bfloat16 [64, 64], P('tensor', 'dp'), may hold values from -3 to 3
- down_weight: bfloat16 [4096, 1024], P('tensor', 'dp'), may hold values from -0.09375 to 0.09375
- down_bias: bfloat16 [1024], P('dp'), may hold values from -3 to 3
Outputs:
- output: float32 [16384, 1024], P(('dp', 'tensor'))
- grad_tokens: float32 [16384, 1024], P(('dp', 'tensor'))
- grad_ln1_gain: float32 [1024], P('dp')
- grad_ln1_bias: float32 [1024], P('dp')
- grad_qkv_weight: float32 [1024, 3, 1024], P('dp', None, 'tensor')
- grad_qkv_bias: float32 [2, 16, 64], P(None, 'tensor', 'dp')
- grad_out_weight: float32 [1024, 1024], P('tensor', 'dp')
- grad_out_bias: float32 [1024], P('dp')
- grad_ln2_gain: float32 [1024], P('dp')
- grad_ln2_bias: float32 [1024], P('dp')
- grad_up_weight: float32 [1024, 4096], P('dp', 'tensor')
- grad_up_bias: float32 [64, 64], P('tensor', 'dp')
- grad_down_weight: float32 [4096, 1024], P('tensor', 'dp')
- grad_down_bias: float32 [1024], P('dp')
Inputs may be any that keep to these rules, and one draw needn't show every extreme that they name: Row g of lengths holds the 8 packed sequences of group g in order; each row sums to 1024 and holds a length of exactly 512.
All inputs are finite; a program needn't handle non-finite values.
Results may differ from a plain program's by a relative error of at most 0.02.
Values may be sent and summed in bfloat16 or wider, within the bound.
No kernel may reach another device: no remote copies, remote signals or barrier semaphores. Data moves between devices by JAX's collectives and lax.ppermute only.
A program may use at most 192 MiB of HBM per device.

v0:
```python
import functools
import math

import jax
import jax.numpy as jnp
from jax import lax
from jax.experimental import pallas as pl
from jax.experimental.pallas import tpu as pltpu
from jax.sharding import PartitionSpec as P

epsilon = 1e-05
gelu_root = math.sqrt(2.0 / math.pi)
gelu_cubic = 0.044715
masked_score = -1e30


def normalize(values, norm_gain, offset):
    center = values - jnp.mean(values, axis=-1, keepdims=True)
    inverse = lax.rsqrt(jnp.mean(center * center, axis=-1, keepdims=True) + epsilon)
    scaled = center * inverse
    return (scaled, inverse, scaled * norm_gain + offset)


def normalize_back(upstream, scaled, inverse, norm_gain):
    weighted = upstream * norm_gain
    return inverse * (
        weighted
        - jnp.mean(weighted, axis=-1, keepdims=True)
        - scaled * jnp.mean(weighted * scaled, axis=-1, keepdims=True)
    )


def gelu_value(values):
    return (
        0.5
        * values
        * (1.0 + jnp.tanh(gelu_root * (values + gelu_cubic * values * values * values)))
    )


def gelu_slope(values):
    tangent = jnp.tanh(gelu_root * (values + gelu_cubic * values * values * values))
    inner_slope = gelu_root * (1.0 + 3.0 * gelu_cubic * values * values)
    return 0.5 * (1.0 + tangent) + 0.5 * values * (1.0 - tangent * tangent) * inner_slope


def contract_rows(left_rows, right_rows):
    return lax.dot_general(
        left_rows, right_rows, (((0,), (0,)), ((), ())), preferred_element_type=jnp.float32
    )


def contract_cols(left_rows, right_rows):
    return lax.dot_general(
        left_rows, right_rows, (((1,), (1,)), ((), ())), preferred_element_type=jnp.float32
    )


def lane_pair(rows, width):
    lane = lax.broadcasted_iota(jnp.int32, rows.shape, 1)
    zero = jnp.zeros_like(rows)
    first = jnp.where(lane < width, rows, zero)
    second = jnp.where(lane < width, zero, rows)
    return jnp.concatenate([first, second], axis=0)


def nt(left, right):
    return lax.dot_general(
        left, right, (((1,), (1,)), ((), ())), preferred_element_type=jnp.float32
    )


def nn(left, right):
    return lax.dot_general(
        left, right, (((1,), (0,)), ((), ())), preferred_element_type=jnp.float32
    )


def tile_pairs(group_rows, block, longest):
    count = group_rows // block
    first = [max(0, (i * block - longest + 1) // block) for i in range(count)]
    return [[j for j in range(first[i], i + 1)] for i in range(count)]


def fill_masks(lengths_ref, mask_ref, tiles, block):
    at = 0
    for i, keys in enumerate(tiles):
        query = i * block + lax.broadcasted_iota(jnp.int32, (1, block), 1)
        start = jnp.zeros((1, block), jnp.int32)
        end = jnp.int32(0)
        for s in range(lengths_ref.shape[1] - 1):
            end = end + lengths_ref[0, s]
            start = jnp.where(query >= end, end, start)
        for j in keys:
            key = j * block + lax.broadcasted_iota(jnp.int32, (block, block), 0)
            allowed = (key >= start) & (key <= query)
            mask_ref[at] = jnp.where(allowed, 0.0, masked_score).astype(jnp.float32)
            at += 1


def unpair(both, block, width):
    own = jnp.concatenate([both[:width, :block], both[width:, block:]], axis=0)
    return own.T


def attention_kernel(lengths_ref, x_ref, o_ref, lse_ref, mask_ref, vt_ref, *, tiles, block, width, scale):
    @pl.when(pl.program_id(0) == 0)
    def _():
        fill_masks(lengths_ref, mask_ref, tiles, block)

    pair = 2 * width
    vt_ref[...] = x_ref[:, 2 * pair : 3 * pair].T
    lse_ref[...] = jnp.zeros_like(lse_ref)
    at = 0
    for i, keys in enumerate(tiles):
        rows = slice(i * block, (i + 1) * block)
        queries = lane_pair(x_ref[rows, :pair], width)
        parts = []
        for t, j in enumerate(keys):
            score = nt(x_ref[j * block : (j + 1) * block, pair : 2 * pair], queries) * scale
            mask = mask_ref[at + t]
            parts.append(score + jnp.concatenate([mask, mask], axis=1))
        at += len(keys)
        peak = parts[0].max(axis=0, keepdims=True)
        for part in parts[1:]:
            peak = jnp.maximum(peak, part.max(axis=0, keepdims=True))
        total = jnp.zeros_like(peak)
        mixed = jnp.zeros((pair, 2 * block), jnp.float32)
        for part, j in zip(parts, keys):
            weight = jnp.exp(part - peak)
            total = total + weight.sum(axis=0, keepdims=True)
            mixed = mixed + nn(vt_ref[:, j * block : (j + 1) * block], weight.astype(jnp.bfloat16))
        o_ref[rows, :] = unpair(mixed / total, block, width).astype(o_ref.dtype)
        log_sum = peak + jnp.log(total)
        lse_ref[0:1, rows] = log_sum[:, :block]
        lse_ref[1:2, rows] = log_sum[:, block:]


def attention_back_kernel(
    lengths_ref, x_ref, o_ref, do_ref, lse_ref, g_ref, sum_ref, mask_ref, kt_ref, dk_ref, dv_ref, *, tiles, block, width, scale
):
    @pl.when(pl.program_id(0) == 0)
    def _():
        fill_masks(lengths_ref, mask_ref, tiles, block)

    pair = 2 * width
    kt_ref[...] = x_ref[:, pair : 2 * pair].T
    dk_ref[...] = jnp.zeros_like(dk_ref)
    dv_ref[...] = jnp.zeros_like(dv_ref)
    query_sum = jnp.zeros((1, pair), jnp.float32)
    at = 0
    for i, keys in enumerate(tiles):
        rows = slice(i * block, (i + 1) * block)
        queries = lane_pair(x_ref[rows, :pair], width)
        upstream = do_ref[rows, :]
        product = (upstream.astype(jnp.float32) * o_ref[rows, :].astype(jnp.float32)).T
        delta = jnp.concatenate(
            [
                product[:width].sum(axis=0, keepdims=True),
                product[width:].sum(axis=0, keepdims=True),
            ],
            axis=1,
        )
        log_sum = jnp.concatenate([lse_ref[0:1, rows], lse_ref[1:2, rows]], axis=1)
        upstream = lane_pair(upstream, width)
        grad_query = jnp.zeros((pair, 2 * block), jnp.float32)
        for j in keys:
            at_keys = slice(j * block, (j + 1) * block)
            score = nt(x_ref[at_keys, pair : 2 * pair], queries) * scale
            mask = mask_ref[at]
            at += 1
            weight = jnp.exp(score + jnp.concatenate([mask, mask], axis=1) - log_sum)
            grad_weight = nt(x_ref[at_keys, 2 * pair : 3 * pair], upstream)
            grad_score = (weight * (grad_weight - delta)).astype(jnp.bfloat16)
            dv_ref[at_keys, :] += nn(weight.astype(jnp.bfloat16), upstream)
            dk_ref[at_keys, :] += nn(grad_score, queries)
            grad_query = grad_query + nn(kt_ref[:, at_keys], grad_score)
        own = unpair(grad_query, block, width) * scale
        query_sum = query_sum + own.sum(axis=0, keepdims=True)
        g_ref[rows, :pair] = own.astype(g_ref.dtype)
    g_ref[:, pair : 2 * pair] = (dk_ref[...] * scale).astype(g_ref.dtype)
    g_ref[:, 2 * pair :] = dv_ref[...].astype(g_ref.dtype)
    sum_ref[...] = jnp.concatenate(
        [query_sum, dv_ref[...].sum(axis=0, keepdims=True), jnp.zeros((6, pair), jnp.float32)], axis=0
    )


def attention(lengths, projected, width):
    group_rows, columns = projected.shape
    pair = 2 * width
    count = columns // (3 * pair)
    block = min(256, group_rows)
    tiles = tile_pairs(group_rows, block, group_rows // 2)
    total = sum(len(keys) for keys in tiles)
    return pl.pallas_call(
        functools.partial(attention_kernel, tiles=tiles, block=block, width=width, scale=width**-0.5),
        out_shape=(
            jax.ShapeDtypeStruct((group_rows, count * pair), jnp.bfloat16),
            jax.ShapeDtypeStruct((count * 8, group_rows), jnp.float32),
        ),
        grid=(count,),
        in_specs=[
            pl.BlockSpec(memory_space=pltpu.SMEM),
            pl.BlockSpec((group_rows, 3 * pair), lambda p: (0, p)),
        ],
        out_specs=(
            pl.BlockSpec((group_rows, pair), lambda p: (0, p)),
            pl.BlockSpec((8, group_rows), lambda p: (p, 0)),
        ),
        scratch_shapes=[
            pltpu.VMEM((total, block, block), jnp.float32),
            pltpu.VMEM((pair, group_rows), jnp.bfloat16),
        ],
        compiler_params=pltpu.CompilerParams(vmem_limit_bytes=56 << 20),
        name="attention",
    )(lengths, projected)


def attention_back(lengths, projected, mixed, grad_mixed, log_sums, width):
    group_rows, columns = projected.shape
    pair = 2 * width
    count = columns // (3 * pair)
    block = min(256, group_rows)
    tiles = tile_pairs(group_rows, block, group_rows // 2)
    total = sum(len(keys) for keys in tiles)
    return pl.pallas_call(
        functools.partial(
            attention_back_kernel, tiles=tiles, block=block, width=width, scale=width**-0.5
        ),
        out_shape=(
            jax.ShapeDtypeStruct((group_rows, columns), jnp.bfloat16),
            jax.ShapeDtypeStruct((8, count * pair), jnp.float32),
        ),
        grid=(count,),
        in_specs=[
            pl.BlockSpec(memory_space=pltpu.SMEM),
            pl.BlockSpec((group_rows, 3 * pair), lambda p: (0, p)),
            pl.BlockSpec((group_rows, pair), lambda p: (0, p)),
            pl.BlockSpec((group_rows, pair), lambda p: (0, p)),
            pl.BlockSpec((8, group_rows), lambda p: (p, 0)),
        ],
        out_specs=(
            pl.BlockSpec((group_rows, 3 * pair), lambda p: (0, p)),
            pl.BlockSpec((8, pair), lambda p: (0, p)),
        ),
        scratch_shapes=[
            pltpu.VMEM((total, block, block), jnp.float32),
            pltpu.VMEM((pair, group_rows), jnp.bfloat16),
            pltpu.VMEM((group_rows, pair), jnp.float32),
            pltpu.VMEM((group_rows, pair), jnp.float32),
        ],
        compiler_params=pltpu.CompilerParams(vmem_limit_bytes=56 << 20),
        name="attention_back",
    )(lengths, projected, mixed, grad_mixed, log_sums)


def tie(*values):
    return lax.optimization_barrier(values)


def flip(value, axis_name, bit):
    size = lax.axis_size(axis_name)
    return lax.ppermute(value, axis_name, [(i, i ^ (1 << bit)) for i in range(size)])


def shift(value, axis_name, step, amount):
    size = lax.axis_size(axis_name)
    return lax.ppermute(value, axis_name, [(i, (i + amount * step) % size) for i in range(size)])


def place_kernel(where_ref, *refs):
    pieces, out_ref, sems = refs[:-2], refs[-2], refs[-1]
    line = pieces[0].shape[0]
    copies = []
    for p, piece in enumerate(pieces):
        for k in range(line):
            at = where_ref[p * line + k]
            copies.append(
                pltpu.make_async_copy(piece.at[k], out_ref.at[at], sems.at[p * line + k])
            )
    for copy in copies:
        copy.start()
    for copy in copies:
        copy.wait()


def place_blocks(pieces, where):
    line, rows, columns = pieces[0].shape
    blocks = line * len(pieces)
    out = pl.pallas_call(
        place_kernel,
        out_shape=jax.ShapeDtypeStruct((blocks, rows, columns), pieces[0].dtype),
        in_specs=[pl.BlockSpec(memory_space=pltpu.SMEM)]
        + [pl.BlockSpec(memory_space=pl.ANY)] * len(pieces),
        out_specs=pl.BlockSpec(memory_space=pltpu.VMEM),
        scratch_shapes=[pltpu.SemaphoreType.DMA((blocks,))],
        name="place_blocks",
    )
    out = out(where, *pieces)
    return out.reshape(blocks * rows, columns)


def gather_line(block):
    line = lax.axis_size("dp") // 4
    return [block] + [shift(block, "dp", 4, k) for k in range(1, line)]


def gather_rest(blocks):
    line = len(blocks)
    own = jnp.stack(blocks)
    side = flip(own, "dp", 1)
    index = lax.axis_index("dp")
    pieces = [own, side] + [flip(half, "dp", 0) for half in (own, side)]
    back = (index // 4 - jnp.arange(line)) % line
    where = jnp.concatenate([back * 4 + ((index % 4) ^ mask) for mask in (0, 2, 1, 3)])
    return place_blocks(pieces, where.astype(jnp.int32))


def pick(values, at, axis):
    return lax.dynamic_index_in_dim(values, at, axis, keepdims=False)


def scatter_core(wholes):
    size = lax.axis_size("dp")
    core = lax.axis_index("dp") % 2
    blocks = [
        whole.reshape(size // 4, 2, 2, whole.shape[0] // size, whole.shape[1]) for whole in wholes
    ]

    def taken(at):
        return jnp.concatenate([pick(block, at, 2) for block in blocks], axis=-1)

    return taken(core), flip(taken(1 - core), "dp", 0)


def scatter_side(kept, met):
    side = (lax.axis_index("dp") // 2) % 2

    def summed(at):
        return pick(kept, at, 1).astype(jnp.float32) + pick(met, at, 1).astype(jnp.float32)

    return summed(side), flip(summed(1 - side).astype(jnp.bfloat16), "dp", 1)


def scatter_line(mine, crossed):
    line = mine.shape[0]
    at = lax.axis_index("dp") // 4
    sums = mine + crossed.astype(jnp.float32)
    low = sums.astype(jnp.bfloat16)
    return [pick(sums, at, 0)] + [
        shift(pick(low, (at + k) % line, 0), "dp", 4, k) for k in range(1, line)
    ]


def total_of(parts):
    return sum(part.astype(jnp.float32) for part in parts)


def bits_of(size):
    count = size.bit_length() - 1
    assert size == 1 << count
    return count


def relative(whole):
    size = lax.axis_size("tensor")
    blocks = whole.reshape((size, whole.shape[0] // size) + whole.shape[1:])
    return [pick(blocks, lax.axis_index("tensor") ^ j, 0) for j in range(size)]


def gather_tensor(block):
    current = block
    for bit in range(bits_of(lax.axis_size("tensor"))):
        current = jnp.concatenate([current, flip(current, "tensor", bit)])
    return current[block.shape[0] :]


def scatter_tensor(own, rest):
    rows = own.shape[0]
    blocks = [own] + [rest[at : at + rows] for at in range(0, rest.shape[0], rows)]
    for bit in reversed(range(bits_of(lax.axis_size("tensor")))):
        half = len(blocks) // 2
        sent = blocks[half:]
        sent = sent[0] if half == 1 else jnp.concatenate(sent)
        met = flip(sent.astype(jnp.bfloat16), "tensor", bit)
        blocks = [
            block + met[j * rows : (j + 1) * rows].astype(jnp.float32)
            for j, block in enumerate(blocks[:half])
        ]
    return blocks[0]


def sum_over(value, axis_name):
    for bit in range(bits_of(lax.axis_size(axis_name))):
        value = value + flip(value, axis_name, bit)
    return value


def as_columns(values, rows):
    flat = values.reshape(-1)
    columns = -(-flat.shape[0] // rows)
    return jnp.pad(flat, (0, columns * rows - flat.shape[0])).reshape(columns, rows)


def block(
    tokens,
    cotangent,
    lengths,
    ln1_gain,
    ln1_bias,
    qkv_weight,
    qkv_bias,
    out_weight,
    out_bias,
    ln2_gain,
    ln2_bias,
    up_weight,
    up_bias,
    down_weight,
    down_bias,
):
    dp, tp = lax.axis_size("dp"), lax.axis_size("tensor")
    local_rows, model_width = tokens.shape
    shard_rows = model_width // dp
    head_local = qkv_bias.shape[1]
    head_width = qkv_bias.shape[2] * dp
    local_width = head_local * head_width
    pairs = head_local // 2
    hidden = up_weight.shape[1]

    vectors = jnp.stack([ln1_gain, ln1_bias, out_bias, ln2_gain, ln2_bias, down_bias])
    qkv_cols = as_columns(qkv_bias, shard_rows)
    up_cols = as_columns(up_bias, shard_rows)
    small = jnp.concatenate([vectors, qkv_cols, up_cols])
    small_width = -(-small.shape[0] // 128) * 128
    small = jnp.pad(small, ((0, small_width - small.shape[0]), (0, 0))).T
    parts = 2 if pairs % 2 == 0 else 1
    part_cols = 3 * local_width // parts
    qkv_shard = (
        qkv_weight.reshape(shard_rows, 3, pairs, 2 * head_width)
        .transpose(0, 2, 1, 3)
        .reshape(shard_rows, parts, part_cols)
    )
    columns = [[qkv_shard[:, part]] for part in range(parts)]
    columns[0].append(small)
    columns[-1].append(out_weight.T)
    shard_list = [jnp.concatenate(piece, axis=1) for piece in columns]
    up_shard, down_shard = up_weight, down_weight.T

    half = local_rows // 2
    rest_rows = [gather_tensor(tokens[:half])]
    lines = [gather_line(shard_list[0])]
    late_tokens, _ = tie(tokens[half:], rest_rows[0])
    for piece in shard_list[1:]:
        piece, *_ = tie(piece, rest_rows[0], *lines[-1])
        lines.append(gather_line(piece))
    rest_rows.append(gather_tensor(late_tokens))
    others = [part.reshape(tp - 1, half, model_width) for part in rest_rows]
    tokens_rest = jnp.concatenate(others, axis=1).reshape((tp - 1) * local_rows, model_width)
    cotangent_late, tokens_rest = tie(cotangent, tokens_rest)
    cotangent_rest = gather_tensor(cotangent_late)

    rest = [gather_rest(lines[0])]
    small_full = rest[0][:, part_cols : part_cols + small_width]

    wide = small_full.astype(jnp.float32).T
    norm1_gain, norm1_offset, out_shift, norm2_gain, norm2_offset, down_shift = (
        wide[i] for i in range(6)
    )
    qkv_at, up_at = 6, 6 + qkv_cols.shape[0]
    up_end = up_at + up_cols.shape[0]

    def from_columns(columns, like):
        count = columns.shape[0]
        blocks = columns.reshape(count, dp, shard_rows).transpose(1, 0, 2).reshape(dp, -1)
        return blocks[:, : like.size].reshape((dp,) + like.shape)

    qkv_bias_full = from_columns(wide[qkv_at:up_at], qkv_bias)
    qkv_bias_full = qkv_bias_full.transpose(1, 2, 0, 3).reshape(2, pairs, 2 * head_width)
    bias_parts = jnp.stack(
        [qkv_bias_full[0], jnp.zeros_like(qkv_bias_full[0]), qkv_bias_full[1]], axis=1
    ).reshape(parts, part_cols)
    up_shift = from_columns(wide[up_at:up_end], up_bias).transpose(1, 0, 2).reshape(hidden)

    token_float = tokens.astype(jnp.float32)
    scaled1, inverse1, pre_own = normalize(token_float, norm1_gain, norm1_offset)
    scaled1_rest, _, pre_rest = normalize(
        tokens_rest.astype(jnp.float32), norm1_gain, norm1_offset
    )
    normed1 = jnp.concatenate(
        relative(jnp.concatenate([pre_own.astype(jnp.bfloat16), pre_rest.astype(jnp.bfloat16)]))
    )

    def project(piece, bias):
        weight = piece[:, :part_cols]
        values = jnp.dot(normed1, weight, preferred_element_type=jnp.float32) + bias
        return weight, values.astype(jnp.bfloat16)

    up_piece, down_piece = up_shard, down_shard
    weight, part = project(rest[0], bias_parts[0])
    up_piece, *_ = tie(up_piece, *lines[-1])
    up_line = gather_line(up_piece)
    qkv_parts, projected = [weight], [part]
    for line, bias in zip(lines[1:], bias_parts[1:]):
        rest.append(gather_rest(line))
        weight, part = project(rest[-1], bias)
        qkv_parts.append(weight)
        projected.append(part)
    out_t = rest[-1][:, -local_width:]
    down_piece, *_ = tie(down_piece, *up_line)
    projected[-1], cotangent_rest = tie(projected[-1], cotangent_rest)
    down_line = gather_line(down_piece)
    attended = []
    for part in projected:
        attended.append(attention(lengths, part, head_width))
    mixed = jnp.concatenate([part[0] for part in attended], axis=1)
    mixed_own, *mixed_rest = relative(mixed)
    mixed_rest = jnp.concatenate(mixed_rest)
    up_full = gather_rest(up_line)
    out_rest = contract_cols(mixed_rest, out_t).astype(jnp.bfloat16)
    (out_own,) = tie(contract_cols(mixed_own, out_t))
    attended_out = scatter_tensor(out_own, out_rest)
    down_t = gather_rest(down_line)
    middle = token_float + attended_out + out_shift

    scaled2, inverse2, pre_two = normalize(middle, norm2_gain, norm2_offset)
    normed2_own = pre_two.astype(jnp.bfloat16)
    normed2_rest = gather_tensor(normed2_own)

    def feed_forward(normed, upstream):
        pre = jnp.dot(normed, up_full, preferred_element_type=jnp.float32) + up_shift
        grad_pre = jnp.dot(upstream, down_t, preferred_element_type=jnp.float32) * gelu_slope(pre)
        low = grad_pre.astype(jnp.bfloat16)
        return gelu_value(pre).astype(jnp.bfloat16), low, jnp.sum(grad_pre, axis=0)

    act_own, pre_own, up_sum_own = tie(*feed_forward(normed2_own, cotangent))
    act_rest, pre_rest, up_sum_rest = tie(*feed_forward(normed2_rest, cotangent_rest))
    grad_up_bias = up_sum_own + up_sum_rest
    norm_rest = contract_cols(pre_rest, up_full).astype(jnp.bfloat16)
    (norm_own,) = tie(contract_cols(pre_own, up_full))
    grad_norm2 = scatter_tensor(norm_own, norm_rest)
    activated = jnp.concatenate([act_own, act_rest])
    grad_pre_low = jnp.concatenate([pre_own, pre_rest])
    cotangent_all = jnp.concatenate([cotangent, cotangent_rest])
    normed2 = jnp.concatenate([normed2_own, normed2_rest])
    grad_down = contract_rows(cotangent_all, activated).astype(jnp.bfloat16)
    grad_up = contract_rows(normed2, grad_pre_low).astype(jnp.bfloat16)
    down_core = scatter_core([grad_down])
    up_core = scatter_core([grad_up])
    grad_down_bias = jnp.sum(cotangent.astype(jnp.float32), axis=0)
    grad_ln2_gain = jnp.sum(grad_norm2 * scaled2, axis=0)
    grad_ln2_bias = jnp.sum(grad_norm2, axis=0)
    grad_middle = cotangent.astype(jnp.float32) + normalize_back(
        grad_norm2, scaled2, inverse2, norm2_gain
    )
    grad_out_bias = jnp.sum(grad_middle, axis=0)
    grad_middle_own = grad_middle.astype(jnp.bfloat16)
    grad_middle_rest = gather_tensor(grad_middle_own)
    down_side = scatter_side(*down_core)
    result_rest = contract_cols(act_rest, down_t).astype(jnp.bfloat16)
    (result_own,) = tie(contract_cols(act_own, down_t))
    feed = scatter_tensor(result_own, result_rest)
    feed, middle_late = tie(feed, middle)
    output = middle_late + feed + down_shift

    grad_middle_all = jnp.concatenate([grad_middle_own, grad_middle_rest])
    grad_mixed = jnp.dot(grad_middle_all, out_t, preferred_element_type=jnp.float32)
    grad_mixed = jnp.concatenate(relative(grad_mixed.astype(jnp.bfloat16)))
    up_side = scatter_side(*up_core)
    width = local_width // parts
    grad_parts, bias_parts = [], []
    down_own = scatter_line(*down_side)
    up_own = None
    for part in range(parts):
        upstream = grad_mixed[:, part * width : (part + 1) * width]
        if part == parts - 1:
            upstream, *up_side = tie(upstream, *up_side)
            up_own = scatter_line(*up_side)
        grads, bias_sums = attention_back(
            lengths, projected[part], attended[part][0], upstream, attended[part][1], head_width
        )
        grad_parts.append(grads)
        bias_parts.append(bias_sums[:2])
    bias_sums = jnp.concatenate(bias_parts, axis=1)
    grad_out_t = contract_rows(
        grad_middle_all, jnp.concatenate([mixed_own, mixed_rest])
    ).astype(jnp.bfloat16)

    def first_grad(blocks):
        return sum(contract_cols(grads, weight) for grads, weight in zip(blocks, qkv_parts))

    by_owner = [relative(grads) for grads in grad_parts]
    part_rest = first_grad([jnp.concatenate(blocks[1:]) for blocks in by_owner])
    (part_own,) = tie(first_grad([blocks[0] for blocks in by_owner]))
    grad_norm1 = scatter_tensor(part_own, part_rest)
    seen_own, seen_rest = tie(part_own, part_rest)
    grad_ln1_gain, grad_ln1_bias = tie(
        jnp.sum(seen_own * scaled1, axis=0) + jnp.sum(seen_rest * scaled1_rest, axis=0),
        jnp.sum(seen_own, axis=0) + jnp.sum(seen_rest, axis=0),
    )
    grad_qkv = []
    for part, grads in enumerate(grad_parts):
        grad_qkv.append(contract_rows(normed1, grads).astype(jnp.bfloat16))

    def to_columns(values, count):
        padded = jnp.pad(values, ((0, 0), (0, count * shard_rows - values.shape[1])))
        return padded.reshape(dp, count, shard_rows).transpose(1, 0, 2).reshape(count, model_width)

    qkv_grads = bias_sums.reshape(2, head_local, dp, -1).transpose(2, 0, 1, 3).reshape(dp, -1)
    up_grads = grad_up_bias.reshape(up_bias.shape[0], dp, -1).transpose(1, 0, 2).reshape(dp, -1)
    sums = jnp.concatenate(
        [
            jnp.stack(
                [
                    grad_ln1_gain,
                    grad_ln1_bias,
                    grad_out_bias,
                    grad_ln2_gain,
                    grad_ln2_bias,
                    grad_down_bias,
                ]
            ),
            to_columns(qkv_grads, up_at - qkv_at),
            to_columns(up_grads, up_end - up_at),
        ]
    ).astype(jnp.bfloat16)
    sums = jnp.pad(sums, ((0, small_width - sums.shape[0]), (0, 0))).T
    pieces = [[part] for part in grad_qkv]
    pieces[0].append(grad_out_t)
    pieces[-1].append(sums)
    own = []
    for piece in pieces:
        core = scatter_core(piece)
        own.append(total_of(scatter_line(*scatter_side(*core))))
    up_shard, down_shard = total_of(up_own), total_of(down_own)
    out_shard = own[0][:, part_cols : part_cols + local_width]
    sums_own = own[-1][:, -small_width:].T[:up_end]
    qkv_shard = (
        jnp.concatenate([piece[:, :part_cols] for piece in own], axis=1)
        .reshape(shard_rows, pairs, 3, 2 * head_width)
        .transpose(0, 2, 1, 3)
        .reshape(shard_rows, 3, local_width)
    )
    vector_sums = sum_over(sums_own[:6], "tensor")
    grad_tokens = grad_middle + normalize_back(grad_norm1, scaled1, inverse1, norm1_gain)
    return (
        output,
        grad_tokens,
        vector_sums[0],
        vector_sums[1],
        qkv_shard,
        sums_own[qkv_at:up_at].reshape(-1)[: qkv_bias.size].reshape(qkv_bias.shape),
        out_shard.T,
        vector_sums[2],
        vector_sums[3],
        vector_sums[4],
        up_shard,
        sums_own[up_at:up_end].reshape(-1)[: up_bias.size].reshape(up_bias.shape),
        down_shard.T,
        vector_sums[5],
    )


def solution(mesh):
    in_specs = (
        P(("dp", "tensor"), None),
        P(("dp", "tensor"), None),
        P("dp", None),
        P("dp"),
        P("dp"),
        P("dp", None, "tensor"),
        P(None, "tensor", "dp"),
        P("tensor", "dp"),
        P("dp"),
        P("dp"),
        P("dp"),
        P("dp", "tensor"),
        P("tensor", "dp"),
        P("tensor", "dp"),
        P("dp"),
    )
    out_specs = (
        P(("dp", "tensor"), None),
        P(("dp", "tensor"), None),
        P("dp"),
        P("dp"),
        P("dp", None, "tensor"),
        P(None, "tensor", "dp"),
        P("tensor", "dp"),
        P("dp"),
        P("dp"),
        P("dp"),
        P("dp", "tensor"),
        P("tensor", "dp"),
        P("tensor", "dp"),
        P("dp"),
    )
    return jax.shard_map(block, mesh=mesh, in_specs=in_specs, out_specs=out_specs, check_vma=False)
```

profile of v0, /device:TPU:0, one launch (start us, length us, event | category | flops | bytes accessed | tf_op | source)
XLA Modules:
  0.0 422.0 jit_solution(7674856114563910233)
XLA Ops:
  5.8 5.1 %collective-permute-start.2 = (bf16[64,896]{1,0:T(8,128)(2,1)}, bf16[64,896]{1,0:T(8,128)(2,1)S(1)}, u32[]{:S(2)}, u32[]{:S(2)}) collective-permute-start(bf16[64,896]{1,0:T(8,128)(2,1)} %get-tuple-element.209), channel_id=1, source_target_pairs={{0,24},{2,26},{4,28},{6,30},{8,0},{10,2},{12,4},{14,6},{16,8},{18,... | collective-permute-start | bytes 344072 | tf_op jit(solution)/shard_map/ppermute | solution.py:268
  15.0 6.1 %collective-permute-done.1 = bf16[64,896]{1,0:T(8,128)(2,1)S(1)} collective-permute-done((bf16[64,896]{1,0:T(8,128)(2,1)}, bf16[64,896]{1,0:T(8,128)(2,1)S(1)}, u32[]{:S(2)}, u32[]{:S(2)}) %collective-permute-start.1) | collective-permute-done | bytes 114720 | tf_op jit(solution)/shard_map/ppermute | solution.py:268
  22.7 2.9 collective-permute-done.6
  25.6 3.1 collective-permute-start.10
  29.8 3.4 collective-permute-done.10
  33.3 9.1 %collective-permute-done.9 = bf16[64,1280]{1,0:T(8,128)(2,1)S(1)} collective-permute-done((bf16[64,1280]{1,0:T(8,128)(2,1)S(1)}, bf16[64,1280]{1,0:T(8,128)(2,1)S(1)}, u32[]{:S(2)}, u32[]{:S(2)}) %collective-permute-start.9) | collective-permute-done | bytes 163872 | tf_op jit(solution)/shard_map/ppermute | solution.py:268
  51.5 15.3 %collective-permute-done.17 = bf16[64,2048]{1,0:T(8,128)(2,1)S(1)} collective-permute-done((bf16[64,2048]{1,0:T(8,128)(2,1)S(1)}, bf16[64,2048]{1,0:T(8,128)(2,1)S(1)}, u32[]{:S(2)}, u32[]{:S(2)}) %collective-permute-start.17) | collective-permute-done | bytes 262176 | tf_op jit(solution)/shard_map/ppermute | solution.py:268
  71.0 3.6 place_blocks.4
  83.2 11.1 %collective-permute-done.23 = bf16[64,2048]{1,0:T(8,128)(2,1)} collective-permute-done((bf16[64,2048]{1,0:T(8,128)(2,1)}, bf16[64,2048]{1,0:T(8,128)(2,1)}, u32[]{:S(2)}, u32[]{:S(2)}) %collective-permute-start.23) | collective-permute-done | bytes 262176 | tf_op jit(solution)/shard_map/ppermute | solution.py:268
  95.9 2.9 add_convert_fusion.1.x_ref
  98.8 7.1 %attention.2 = (bf16[1024,256]{1,0:T(8,128)(2,1)}, f32[16,1024]{1,0:T(8,128)}) custom-call(s32[1,8]{1,0:T(1,128)} %lengths_ref.7, bf16[1024,768]{1,0:T(8,128)(2,1)} %add_convert_fusion.1.x_ref), custom_call_target="tpu_custom_call" | custom-call | tf_op jit(solution)/shard_map/attention/pallas_call | solution.py:195
  109.6 4.1 place_blocks.5
  113.7 5.0 %add_convert_fusion.x_ref = bf16[1024,768]{1,0:T(8,128)(2,1)} fusion(f32[768]{0:T(1024)S(1)} %add.522, bf16[1024,1280]{1,0:T(8,128)(2,1)} %bitcast.287, bf16[512,1024]{1,0:T(8,128)(2,1)} %copy-done.30, bf16[512,1024]{1,0:T(8,128)(2,1)} %copy-done.28), kind=kOutput, calls=%fused_computation.30 | convolution fusion | flops 1616379904 | bytes 5245952 | tf_op jit(solution)/shard_map/dot_general | solution.py:496
  118.8 7.4 %attention.3 = (bf16[1024,256]{1,0:T(8,128)(2,1)}, f32[16,1024]{1,0:T(8,128)}) custom-call(s32[1,8]{1,0:T(1,128)} %lengths_ref.7, bf16[1024,768]{1,0:T(8,128)(2,1)} %add_convert_fusion.x_ref), custom_call_target="tpu_custom_call" | custom-call | tf_op jit(solution)/shard_map/attention/pallas_call | solution.py:195
  129.0 2.9 convolution_convert_fusion.4
  135.6 3.4 fusion.75
  139.6 5.0 %place_blocks.6 = bf16[16,64,2048]{2,1,0:T(8,128)(2,1)} custom-call(s32[16]{0:T(128)} %pad_add_fusion.where_ref, bf16[4,64,2048]{2,1,0:T(8,128)(2,1)} %copy-done.13, bf16[4,64,2048]{2,1,0:T(8,128)(2,1)} %collective-permute-done.19.refs_1_, bf16[4,64,2048]{2,1,0:T(8,128)(2,1)} %collective-permute-done.20.refs_2_, ...), custom_call_target="tpu_custom_call" | custom-call | tf_op jit(solution)/shard_map/place_blocks/pallas_call | solution.py:299
  144.5 13.2 %collective-permute-done.15 = bf16[512,1024]{1,0:T(8,128)(2,1)} collective-permute-done((bf16[512,1024]{1,0:T(8,128)(2,1)}, bf16[512,1024]{1,0:T(8,128)(2,1)}, u32[]{:S(2)}, u32[]{:S(2)}) %collective-permute-start.15) | collective-permute-done | bytes 1048608 | tf_op jit(solution)/shard_map/ppermute | solution.py:263
  162.7 5.6 %fusion.134 = f32[512,2048]{1,0:T(8,128)} fusion(bf16[512,1024]{1,0:T(8,128)(2,1)} %add_convert_fusion.2, bf16[1024,2048]{1,0:T(8,128)(2,1)S(1)} %bitcast.294), kind=kOutput, calls=%fused_computation.270 | convolution fusion | flops 2147483648 | bytes 9437184 | tf_op jit(solution)/shard_map/dot_general | solution.py:531
  168.3 5.0 %place_blocks.7 = bf16[16,64,2048]{2,1,0:T(8,128)(2,1)} custom-call(s32[16]{0:T(128)} %pad_add_fusion.where_ref, bf16[4,64,2048]{2,1,0:T(8,128)(2,1)} %pad_maximum_fusion.8.refs_0_, bf16[4,64,2048]{2,1,0:T(8,128)(2,1)} %collective-permute-done.25.refs_1_, bf16[4,64,2048]{2,1,0:T(8,128)(2,1)} %collective-permute-done.26.refs_2_, ...), custom_call_target="tpu_custom_call" | custom-call | tf_op jit(solution)/shard_map/place_blocks/pallas_call | solution.py:299
  173.3 9.7 %fusion.127 = (f32[2048]{0:T(1024)S(1)}, bf16[512,2048]{1,0:T(8,128)(2,1)}) fusion(f32[512,2048]{1,0:T(8,128)} %fusion.134, f32[2048]{0:T(1024)S(1)} %add.534, bf16[512,1024]{1,0:T(8,128)(2,1)} %param.16, bf16[1024,2048]{1,0:T(8,128)(2,1)} %bitcast.297), kind=kOutput, calls=%fused_computation.263 | convolution fusion | flops 2169501696 | bytes 11550720 | tf_op jit(solution)/shard_map/dot_general | solution.py:532
  183.0 3.9 collective-permute-done.28
  186.9 6.5 %multiply_convert_fusion = (bf16[512,2048]{1,0:T(8,128)(2,1)S(1)}, bf16[512,2048]{1,0:T(8,128)(2,1)S(1)}, f32[512,2048]{1,0:T(8,128)S(1)}) fusion(f32[2048]{0:T(1024)S(1)} %add.534, f32[512,2048]{1,0:T(8,128)S(1)} %copy-done.53, bf16[512,1024]{1,0:T(8,128)(2,1)} %collective-permute-done.28, bf16[1024,2048]{1,0:T(8,128)(2,1)S(1)} %bitcast.295), kind=kOutput, calls=%fused_computation.26 | convolution fusion | flops 2168455168 | bytes 17833984 | tf_op jit(solution)/shard_map/dot_general | solution.py:531
  193.4 3.7 fusion.135
  197.1 6.9 %fusion.126 = (f32[2048]{0:T(1024)S(1)}, bf16[512,2048]{1,0:T(8,128)(2,1)}) fusion(f32[512,2048]{1,0:T(8,128)S(1)} %get-tuple-element.216, f32[2048]{0:T(1024)S(1)} %add.534, bf16[512,1024]{1,0:T(8,128)(2,1)} %collective-permute-done.14, bf16[1024,2048]{1,0:T(8,128)(2,1)S(1)} %bitcast.299), kind=kOutput, calls=%fused_computation.262 | convolution fusion | flops 2169501696 | bytes 11550720 | tf_op jit(solution)/shard_map/dot_general | solution.py:532
  204.0 3.4 convolution_convert_fusion.6
  207.4 7.6 %fusion.22 = bf16[1024,2048]{1,0:T(8,128)(2,1)} fusion(bf16[512,2048]{1,0:T(8,128)(2,1)S(1)} %get-tuple-element.56, bf16[512,2048]{1,0:T(8,128)(2,1)S(1)} %get-tuple-element.54, bf16[512,1024]{1,0:T(8,128)(2,1)} %collective-permute-done.14, bf16[512,1024]{1,0:T(8,128)(2,1)S(1)} %copy-done.11), kind=kOutput, calls=%fused_computation.28 | convolution fusion | flops 4309647360 | bytes 10485760 | tf_op jit(solution)/shard_map/dot_general | solution.py:48
  216.4 5.3 %convolution_convert_fusion.5 = bf16[512,1024]{1,0:T(8,128)(2,1)S(1)} fusion(bf16[512,2048]{1,0:T(8,128)(2,1)} %get-tuple-element.60, bf16[1024,2048]{1,0:T(8,128)(2,1)} %bitcast.293), kind=kOutput, calls=%fused_computation.99 | convolution fusion | flops 2148007936 | bytes 7340032 | tf_op jit(solution)/shard_map/dot_general | solution.py:54
  227.9 6.6 %fusion.25 = bf16[1024,2048]{1,0:T(8,128)(2,1)S(1)} fusion(bf16[512,2048]{1,0:T(8,128)(2,1)S(1)} %copy-done.55, bf16[512,2048]{1,0:T(8,128)(2,1)S(1)} %copy-done.54, bf16[512,1024]{1,0:T(8,128)(2,1)} %collective-permute-done.28, bf16[512,1024]{1,0:T(8,128)(2,1)} %add_convert_fusion.2), kind=kOutput, calls=%fused_computation.29 | convolution fusion | flops 4309647360 | bytes 10485760 | tf_op jit(solution)/shard_map/dot_general | solution.py:48
  234.7 15.5 %collective-permute-done.30 = bf16[512,1024]{1,0:T(8,128)(2,1)S(1)} collective-permute-done((bf16[512,1024]{1,0:T(8,128)(2,1)S(1)}, bf16[512,1024]{1,0:T(8,128)(2,1)S(1)}, u32[]{:S(2)}, u32[]{:S(2)}) %collective-permute-start.30) | collective-permute-done | bytes 1048608 | tf_op jit(solution)/shard_map/ppermute | solution.py:263
  252.9 19.8 %collective-permute-done.29 = bf16[512,1024]{1,0:T(8,128)(2,1)S(1)} collective-permute-done((bf16[512,1024]{1,0:T(8,128)(2,1)S(1)}, bf16[512,1024]{1,0:T(8,128)(2,1)S(1)}, u32[]{:S(2)}, u32[]{:S(2)}) %collective-permute-start.29) | collective-permute-done | bytes 1048608 | tf_op jit(solution)/shard_map/ppermute | solution.py:263
  282.2 10.8 %collective-permute-done.31 = bf16[512,1024]{1,0:T(8,128)(2,1)S(1)} collective-permute-done((bf16[512,1024]{1,0:T(8,128)(2,1)S(1)}, bf16[512,1024]{1,0:T(8,128)(2,1)S(1)}, u32[]{:S(2)}, u32[]{:S(2)}) %collective-permute-start.31) | collective-permute-done | bytes 1048608 | tf_op jit(solution)/shard_map/ppermute | solution.py:263
  300.0 9.5 %attention_back.2 = (bf16[1024,768]{1,0:T(8,128)(2,1)}, f32[8,256]{1,0:T(8,128)}) custom-call(s32[1,8]{1,0:T(1,128)} %lengths_ref.7, bf16[1024,768]{1,0:T(8,128)(2,1)} %add_convert_fusion.1.x_ref, bf16[1024,256]{1,0:T(8,128)(2,1)} %get-tuple-element.47.o_ref, bf16[1024,256]{1,0:T(8,128)(2,1)} %get-tuple-element.181.do_ref, f32[16,1024]{1,0:T(8,128)} %get-tuple-element.61.lse_ref), custom_call_target="tpu_custom_call" | custom-call | tf_op jit(solution)/shard_map/attention_back/pallas_call | solution.py:226
  311.7 3.1 convolution_convert_fusion
  316.2 5.8 %collective-permute-done.33 = bf16[4,64,2048]{2,1,0:T(8,128)(2,1)} collective-permute-done((bf16[4,64,2048]{2,1,0:T(8,128)(2,1)}, bf16[4,64,2048]{2,1,0:T(8,128)(2,1)}, u32[]{:S(2)}, u32[]{:S(2)}) %collective-permute-start.33) | collective-permute-done | bytes 1048608 | tf_op jit(solution)/shard_map/ppermute | solution.py:263
  322.0 9.1 %attention_back.3 = (bf16[1024,768]{1,0:T(8,128)(2,1)}, f32[8,256]{1,0:T(8,128)}) custom-call(s32[1,8]{1,0:T(1,128)} %lengths_ref.7, bf16[1024,768]{1,0:T(8,128)(2,1)} %add_convert_fusion.x_ref, bf16[1024,256]{1,0:T(8,128)(2,1)} %get-tuple-element.51.o_ref, bf16[1024,256]{1,0:T(8,128)(2,1)} %get-tuple-element.63.do_ref, f32[16,1024]{1,0:T(8,128)} %get-tuple-element.64.lse_ref), custom_call_target="tpu_custom_call" | custom-call | tf_op jit(solution)/shard_map/attention_back/pallas_call | solution.py:226
  336.6 3.6 fusion.118
  341.2 4.1 collective-permute-start.53
  346.0 2.7 fusion.133
  349.0 3.0 fusion.120
  360.2 3.2 collective-permute-start.48
  363.4 8.7 %collective-permute-done.52 = bf16[64,2048]{1,0:T(8,128)(2,1)} collective-permute-done((bf16[64,2048]{1,0:T(8,128)(2,1)}, bf16[64,2048]{1,0:T(8,128)(2,1)}, u32[]{:S(2)}, u32[]{:S(2)}) %collective-permute-start.52) | collective-permute-done | bytes 262176 | tf_op jit(solution)/shard_map/ppermute | solution.py:268
  379.4 3.3 fusion.117
  384.0 3.4 collective-permute-done.42
  388.8 3.7 collective-permute-start.43
  399.6 4.8 %collective-permute-done.44 = bf16[64,1280]{1,0:T(8,128)(2,1)S(1)} collective-permute-done((bf16[64,1280]{1,0:T(8,128)(2,1)S(1)}, bf16[64,1280]{1,0:T(8,128)(2,1)S(1)}, u32[]{:S(2)}, u32[]{:S(2)}) %collective-permute-start.44) | collective-permute-done | bytes 163872 | tf_op jit(solution)/shard_map/ppermute | solution.py:268
  406.1 3.3 collective-permute-start.39
  412.3 4.3 %collective-permute-done.38 = bf16[64,896]{1,0:T(8,128)(2,1)S(1)} collective-permute-done((bf16[64,896]{1,0:T(8,128)(2,1)S(1)}, bf16[64,896]{1,0:T(8,128)(2,1)S(1)}, u32[]{:S(2)}, u32[]{:S(2)}) %collective-permute-start.38) | collective-permute-done | bytes 114720 | tf_op jit(solution)/shard_map/ppermute | solution.py:268
  (346 shorter events, 122.8 us)
Async XLA Ops:
  5.8 9.2 %collective-permute-start.2 = (bf16[64,896]{1,0:T(8,128)(2,1)}, bf16[64,896]{1,0:T(8,128)(2,1)S(1)}, u32[]{:S(2)}, u32[]{:S(2)}) collective-permute-start(bf16[64,896]{1,0:T(8,128)(2,1)} %get-tuple-element.209), channel_id=1, source_target_pairs={{0,24},{2,26},{4,28},{6,30},{8,0},{10,2},{12,4},{14,6},{16,8},{18,... | collective-permute-start | bytes 344072 | tf_op jit(solution)/shard_map/ppermute | solution.py:268
  10.9 10.2 %collective-permute-start.1 = (bf16[64,896]{1,0:T(8,128)(2,1)}, bf16[64,896]{1,0:T(8,128)(2,1)S(1)}, u32[]{:S(2)}, u32[]{:S(2)}) collective-permute-start(bf16[64,896]{1,0:T(8,128)(2,1)} %get-tuple-element.209), channel_id=1, source_target_pairs={{0,16},{2,18},{4,20},{6,22},{8,24},{10,26},{12,28},{14,30},{16,0},... | collective-permute-start | bytes 344072 | tf_op jit(solution)/shard_map/ppermute | solution.py:268
  10.9 10.2 %collective-permute-start = (bf16[64,896]{1,0:T(8,128)(2,1)}, bf16[64,896]{1,0:T(8,128)(2,1)S(1)}, u32[]{:S(2)}, u32[]{:S(2)}) collective-permute-start(bf16[64,896]{1,0:T(8,128)(2,1)} %get-tuple-element.209), channel_id=1, source_target_pairs={{0,8},{2,10},{4,12},{6,14},{8,16},{10,18},{12,20},{14,22},{16,24},... | collective-permute-start | bytes 344072 | tf_op jit(solution)/shard_map/ppermute | solution.py:268
  12.8 12.8 %collective-permute-start.6 = (bf16[256,1024]{1,0:T(8,128)(2,1)S(1)}, bf16[256,1024]{1,0:T(8,128)(2,1)S(1)}, u32[]{:S(2)}, u32[]{:S(2)}) collective-permute-start(bf16[256,1024]{1,0:T(8,128)(2,1)S(1)} %get-tuple-element.188), channel_id=1, source_target_pairs={{0,1},{1,0},{2,3},{3,2},{4,5},{5,4},{6,7},{7,6},{8,9},{9,8},{10,11... | collective-permute-start | bytes 1572872 | tf_op jit(solution)/shard_map/ppermute | solution.py:263
  21.2 25.7 %collective-permute-start.3 = (bf16[4,64,896]{2,1,0:T(8,128)(2,1)S(1)}, bf16[4,64,896]{2,1,0:T(8,128)(2,1)}, u32[]{:S(2)}, u32[]{:S(2)}) collective-permute-start(bf16[4,64,896]{2,1,0:T(8,128)(2,1)S(1)} %pad_maximum_fusion.12.refs_0_), channel_id=1, source_target_pairs={{0,4},{2,6},{4,0},{6,2},{8,12},{10,14},{12,8},{14,10},{16,20},{18,... | collective-permute-start | bytes 1376264 | tf_op jit(solution)/shard_map/ppermute | solution.py:263
  25.6 7.7 %collective-permute-start.10 = (bf16[64,1280]{1,0:T(8,128)(2,1)S(1)}, bf16[64,1280]{1,0:T(8,128)(2,1)S(1)}, u32[]{:S(2)}, u32[]{:S(2)}) collective-permute-start(bf16[64,1280]{1,0:T(8,128)(2,1)S(1)} %pad_maximum_fusion.14), channel_id=1, source_target_pairs={{0,24},{2,26},{4,28},{6,30},{8,0},{10,2},{12,4},{14,6},{16,8},{18,... | collective-permute-start | bytes 491528 | tf_op jit(solution)/shard_map/ppermute | solution.py:268
  28.7 13.7 %collective-permute-start.9 = (bf16[64,1280]{1,0:T(8,128)(2,1)S(1)}, bf16[64,1280]{1,0:T(8,128)(2,1)S(1)}, u32[]{:S(2)}, u32[]{:S(2)}) collective-permute-start(bf16[64,1280]{1,0:T(8,128)(2,1)S(1)} %pad_maximum_fusion.14), channel_id=1, source_target_pairs={{0,16},{2,18},{4,20},{6,22},{8,24},{10,26},{12,28},{14,30},{16,0},... | collective-permute-start | bytes 491528 | tf_op jit(solution)/shard_map/ppermute | solution.py:268
  29.5 13.5 %collective-permute-start.8 = (bf16[64,1280]{1,0:T(8,128)(2,1)S(1)}, bf16[64,1280]{1,0:T(8,128)(2,1)}, u32[]{:S(2)}, u32[]{:S(2)}) collective-permute-start(bf16[64,1280]{1,0:T(8,128)(2,1)S(1)} %pad_maximum_fusion.14), channel_id=1, source_target_pairs={{0,8},{2,10},{4,12},{6,14},{8,16},{10,18},{12,20},{14,22},{16,24},... | collective-permute-start | bytes 491528 | tf_op jit(solution)/shard_map/ppermute | solution.py:268
  43.0 23.7 %collective-permute-start.17 = (bf16[64,2048]{1,0:T(8,128)(2,1)S(1)}, bf16[64,2048]{1,0:T(8,128)(2,1)S(1)}, u32[]{:S(2)}, u32[]{:S(2)}) collective-permute-start(bf16[64,2048]{1,0:T(8,128)(2,1)S(1)} %copy-done.37), channel_id=1, source_target_pairs={{0,16},{2,18},{4,20},{6,22},{8,24},{10,26},{12,28},{14,30},{16,0},... | collective-permute-start | bytes 786440 | tf_op jit(solution)/shard_map/ppermute | solution.py:268
  44.2 22.6 %collective-permute-start.16 = (bf16[64,2048]{1,0:T(8,128)(2,1)S(1)}, bf16[64,2048]{1,0:T(8,128)(2,1)S(1)}, u32[]{:S(2)}, u32[]{:S(2)}) collective-permute-start(bf16[64,2048]{1,0:T(8,128)(2,1)S(1)} %copy-done.37), channel_id=1, source_target_pairs={{0,8},{2,10},{4,12},{6,14},{8,16},{10,18},{12,20},{14,22},{16,24},... | collective-permute-start | bytes 786440 | tf_op jit(solution)/shard_map/ppermute | solution.py:268
  46.9 22.8 %collective-permute-start.4 = (bf16[4,64,896]{2,1,0:T(8,128)(2,1)S(1)}, bf16[4,64,896]{2,1,0:T(8,128)(2,1)S(1)}, u32[]{:S(2)}, u32[]{:S(2)}) collective-permute-start(bf16[4,64,896]{2,1,0:T(8,128)(2,1)S(1)} %pad_maximum_fusion.12.refs_0_), channel_id=1, source_target_pairs={{0,2},{2,0},{4,6},{6,4},{8,10},{10,8},{12,14},{14,12},{16,18},{18,... | collective-permute-start | bytes 1376264 | tf_op jit(solution)/shard_map/ppermute | solution.py:263
  46.9 23.6 %collective-permute-start.5 = (bf16[4,64,896]{2,1,0:T(8,128)(2,1)}, bf16[4,64,896]{2,1,0:T(8,128)(2,1)}, u32[]{:S(2)}, u32[]{:S(2)}) collective-permute-start(bf16[4,64,896]{2,1,0:T(8,128)(2,1)} %collective-permute-done.3.refs_1_), channel_id=1, source_target_pairs={{0,2},{2,0},{4,6},{6,4},{8,10},{10,8},{12,14},{14,12},{16,18},{18,... | collective-permute-start | bytes 1376264 | tf_op jit(solution)/shard_map/ppermute | solution.py:263
  50.0 26.3 %collective-permute-start.7 = (bf16[256,1024]{1,0:T(8,128)(2,1)}, bf16[256,1024]{1,0:T(8,128)(2,1)}, u32[]{:S(2)}, u32[]{:S(2)}) collective-permute-start(bf16[256,1024]{1,0:T(8,128)(2,1)} %get-tuple-element.45), channel_id=1, source_target_pairs={{0,1},{1,0},{2,3},{3,2},{4,5},{5,4},{6,7},{7,6},{8,9},{9,8},{10,11... | collective-permute-start | bytes 1572872 | tf_op jit(solution)/shard_map/ppermute | solution.py:263
  66.8 41.8 %collective-permute-start.12 = (bf16[4,64,1280]{2,1,0:T(8,128)(2,1)}, bf16[4,64,1280]{2,1,0:T(8,128)(2,1)}, u32[]{:S(2)}, u32[]{:S(2)}) collective-permute-start(bf16[4,64,1280]{2,1,0:T(8,128)(2,1)} %pad_maximum_fusion.10.refs_0_), channel_id=1, source_target_pairs={{0,2},{2,0},{4,6},{6,4},{8,10},{10,8},{12,14},{14,12},{16,18},{18,... | collective-permute-start | bytes 1966088 | tf_op jit(solution)/shard_map/ppermute | solution.py:263
  66.8 29.0 %collective-permute-start.11 = (bf16[4,64,1280]{2,1,0:T(8,128)(2,1)}, bf16[4,64,1280]{2,1,0:T(8,128)(2,1)}, u32[]{:S(2)}, u32[]{:S(2)}) collective-permute-start(bf16[4,64,1280]{2,1,0:T(8,128)(2,1)} %pad_maximum_fusion.10.refs_0_), channel_id=1, source_target_pairs={{0,4},{2,6},{4,0},{6,2},{8,12},{10,14},{12,8},{14,10},{16,20},{18,... | collective-permute-start | bytes 1966088 | tf_op jit(solution)/shard_map/ppermute | solution.py:263
  70.4 9.9 %collective-permute-start.24 = (bf16[64,2048]{1,0:T(8,128)(2,1)}, bf16[64,2048]{1,0:T(8,128)(2,1)S(1)}, u32[]{:S(2)}, u32[]{:S(2)}) collective-permute-start(bf16[64,2048]{1,0:T(8,128)(2,1)} %bitcast.327), channel_id=1, source_target_pairs={{0,24},{2,26},{4,28},{6,30},{8,0},{10,2},{12,4},{14,6},{16,8},{18,... | collective-permute-start | bytes 786440 | tf_op jit(solution)/shard_map/ppermute | solution.py:268
  70.5 23.9 %collective-permute-start.23 = (bf16[64,2048]{1,0:T(8,128)(2,1)}, bf16[64,2048]{1,0:T(8,128)(2,1)}, u32[]{:S(2)}, u32[]{:S(2)}) collective-permute-start(bf16[64,2048]{1,0:T(8,128)(2,1)} %bitcast.328), channel_id=1, source_target_pairs={{0,16},{2,18},{4,20},{6,22},{8,24},{10,26},{12,28},{14,30},{16,0},... | collective-permute-start | bytes 786440 | tf_op jit(solution)/shard_map/ppermute | solution.py:268
  76.3 33.3 %collective-permute-start.19 = (bf16[4,64,2048]{2,1,0:T(8,128)(2,1)S(1)}, bf16[4,64,2048]{2,1,0:T(8,128)(2,1)}, u32[]{:S(2)}, u32[]{:S(2)}) collective-permute-start(bf16[4,64,2048]{2,1,0:T(8,128)(2,1)S(1)} %pad_maximum_fusion.7.refs_0_), channel_id=1, source_target_pairs={{0,4},{2,6},{4,0},{6,2},{8,12},{10,14},{12,8},{14,10},{16,20},{18,... | collective-permute-start | bytes 3145736 | tf_op jit(solution)/shard_map/ppermute | solution.py:263
  81.0 24.9 %collective-permute-start.22 = (bf16[64,2048]{1,0:T(8,128)(2,1)S(1)}, bf16[64,2048]{1,0:T(8,128)(2,1)S(1)}, u32[]{:S(2)}, u32[]{:S(2)}) collective-permute-start(bf16[64,2048]{1,0:T(8,128)(2,1)S(1)} %bitcast.329), channel_id=1, source_target_pairs={{0,8},{2,10},{4,12},{6,14},{8,16},{10,18},{12,20},{14,22},{16,24},... | collective-permute-start | bytes 786440 | tf_op jit(solution)/shard_map/ppermute | solution.py:268
  94.3 24.4 %collective-permute-start.14 = (bf16[512,1024]{1,0:T(8,128)(2,1)S(1)}, bf16[512,1024]{1,0:T(8,128)(2,1)}, u32[]{:S(2)}, u32[]{:S(2)}) collective-permute-start(bf16[512,1024]{1,0:T(8,128)(2,1)S(1)} %copy-done.10), channel_id=1, source_target_pairs={{0,1},{1,0},{2,3},{3,2},{4,5},{5,4},{6,7},{7,6},{8,9},{9,8},{10,11... | collective-permute-start | bytes 3145736 | tf_op jit(solution)/shard_map/ppermute | solution.py:263
  95.9 13.8 %collective-permute-start.13 = (bf16[4,64,1280]{2,1,0:T(8,128)(2,1)}, bf16[4,64,1280]{2,1,0:T(8,128)(2,1)}, u32[]{:S(2)}, u32[]{:S(2)}) collective-permute-start(bf16[4,64,1280]{2,1,0:T(8,128)(2,1)} %collective-permute-done.11.refs_1_), channel_id=1, source_target_pairs={{0,2},{2,0},{4,6},{6,4},{8,10},{10,8},{12,14},{14,12},{16,18},{18,... | collective-permute-start | bytes 1966088 | tf_op jit(solution)/shard_map/ppermute | solution.py:263
  105.9 33.6 %collective-permute-start.20 = (bf16[4,64,2048]{2,1,0:T(8,128)(2,1)S(1)}, bf16[4,64,2048]{2,1,0:T(8,128)(2,1)}, u32[]{:S(2)}, u32[]{:S(2)}) collective-permute-start(bf16[4,64,2048]{2,1,0:T(8,128)(2,1)S(1)} %pad_maximum_fusion.7.refs_0_), channel_id=1, source_target_pairs={{0,2},{2,0},{4,6},{6,4},{8,10},{10,8},{12,14},{14,12},{16,18},{18,... | collective-permute-start | bytes 3145736 | tf_op jit(solution)/shard_map/ppermute | solution.py:263
  108.6 30.4 %collective-permute-start.25 = (bf16[4,64,2048]{2,1,0:T(8,128)(2,1)}, bf16[4,64,2048]{2,1,0:T(8,128)(2,1)}, u32[]{:S(2)}, u32[]{:S(2)}) collective-permute-start(bf16[4,64,2048]{2,1,0:T(8,128)(2,1)} %pad_maximum_fusion.8.refs_0_), channel_id=1, source_target_pairs={{0,4},{2,6},{4,0},{6,2},{8,12},{10,14},{12,8},{14,10},{16,20},{18,... | collective-permute-start | bytes 3145736 | tf_op jit(solution)/shard_map/ppermute | solution.py:263
  109.6 29.9 %collective-permute-start.21 = (bf16[4,64,2048]{2,1,0:T(8,128)(2,1)}, bf16[4,64,2048]{2,1,0:T(8,128)(2,1)}, u32[]{:S(2)}, u32[]{:S(2)}) collective-permute-start(bf16[4,64,2048]{2,1,0:T(8,128)(2,1)} %collective-permute-done.19.refs_1_), channel_id=1, source_target_pairs={{0,2},{2,0},{4,6},{6,4},{8,10},{10,8},{12,14},{14,12},{16,18},{18,... | collective-permute-start | bytes 3145736 | tf_op jit(solution)/shard_map/ppermute | solution.py:263
  131.9 25.9 %collective-permute-start.15 = (bf16[512,1024]{1,0:T(8,128)(2,1)}, bf16[512,1024]{1,0:T(8,128)(2,1)}, u32[]{:S(2)}, u32[]{:S(2)}) collective-permute-start(bf16[512,1024]{1,0:T(8,128)(2,1)} %convolution_convert_fusion.4), channel_id=1, source_target_pairs={{0,1},{1,0},{2,3},{3,2},{4,5},{5,4},{6,7},{7,6},{8,9},{9,8},{10,11... | collective-permute-start | bytes 3145736 | tf_op jit(solution)/shard_map/ppermute | solution.py:263
  135.5 32.7 %collective-permute-start.26 = (bf16[4,64,2048]{2,1,0:T(8,128)(2,1)}, bf16[4,64,2048]{2,1,0:T(8,128)(2,1)}, u32[]{:S(2)}, u32[]{:S(2)}) collective-permute-start(bf16[4,64,2048]{2,1,0:T(8,128)(2,1)} %pad_maximum_fusion.8.refs_0_), channel_id=1, source_target_pairs={{0,2},{2,0},{4,6},{6,4},{8,10},{10,8},{12,14},{14,12},{16,18},{18,... | collective-permute-start | bytes 3145736 | tf_op jit(solution)/shard_map/ppermute | solution.py:263
  139.1 29.2 %collective-permute-start.27 = (bf16[4,64,2048]{2,1,0:T(8,128)(2,1)}, bf16[4,64,2048]{2,1,0:T(8,128)(2,1)}, u32[]{:S(2)}, u32[]{:S(2)}) collective-permute-start(bf16[4,64,2048]{2,1,0:T(8,128)(2,1)} %collective-permute-done.25.refs_1_), channel_id=1, source_target_pairs={{0,2},{2,0},{4,6},{6,4},{8,10},{10,8},{12,14},{14,12},{16,18},{18,... | collective-permute-start | bytes 3145736 | tf_op jit(solution)/shard_map/ppermute | solution.py:263
  161.9 25.0 %collective-permute-start.28 = (bf16[512,1024]{1,0:T(8,128)(2,1)}, bf16[512,1024]{1,0:T(8,128)(2,1)}, u32[]{:S(2)}, u32[]{:S(2)}) collective-permute-start(bf16[512,1024]{1,0:T(8,128)(2,1)} %add_convert_fusion.2), channel_id=1, source_target_pairs={{0,1},{1,0},{2,3},{3,2},{4,5},{5,4},{6,7},{7,6},{8,9},{9,8},{10,11... | collective-permute-start | bytes 3145736 | tf_op jit(solution)/shard_map/ppermute | solution.py:263
  224.2 26.1 %collective-permute-start.30 = (bf16[512,1024]{1,0:T(8,128)(2,1)S(1)}, bf16[512,1024]{1,0:T(8,128)(2,1)S(1)}, u32[]{:S(2)}, u32[]{:S(2)}) collective-permute-start(bf16[512,1024]{1,0:T(8,128)(2,1)S(1)} %convolution_convert_fusion.5), channel_id=1, source_target_pairs={{0,1},{1,0},{2,3},{3,2},{4,5},{5,4},{6,7},{7,6},{8,9},{9,8},{10,11... | collective-permute-start | bytes 3145736 | tf_op jit(solution)/shard_map/ppermute | solution.py:263
  224.5 48.2 %collective-permute-start.29 = (bf16[512,1024]{1,0:T(8,128)(2,1)S(1)}, bf16[512,1024]{1,0:T(8,128)(2,1)S(1)}, u32[]{:S(2)}, u32[]{:S(2)}) collective-permute-start(bf16[512,1024]{1,0:T(8,128)(2,1)S(1)} %copy-done.52), channel_id=1, source_target_pairs={{0,1},{1,0},{2,3},{3,2},{4,5},{5,4},{6,7},{7,6},{8,9},{9,8},{10,11... | collective-permute-start | bytes 3145736 | tf_op jit(solution)/shard_map/ppermute | solution.py:263
  226.5 50.2 %collective-permute-start.49 = (bf16[4,2,64,2048]{3,2,0,1:T(8,128)(2,1)S(1)}, bf16[4,2,64,2048]{3,2,0,1:T(8,128)(2,1)S(1)}, u32[]{:S(2)}, u32[]{:S(2)}) collective-permute-start(bf16[4,2,64,2048]{3,2,0,1:T(8,128)(2,1)S(1)} %copy_bitcast_fusion), channel_id=1, source_target_pairs={{0,2},{2,0},{4,6},{6,4},{8,10},{10,8},{12,14},{14,12},{16,18},{18,... | collective-permute-start | bytes 6291464 | tf_op jit(solution)/shard_map/ppermute | solution.py:263
  234.6 44.8 %collective-permute-start.32 = (bf16[4,2,64,2048]{3,2,0,1:T(8,128)(2,1)S(1)}, bf16[4,2,64,2048]{3,2,0,1:T(8,128)(2,1)S(1)}, u32[]{:S(2)}, u32[]{:S(2)}) collective-permute-start(bf16[4,2,64,2048]{3,2,0,1:T(8,128)(2,1)S(1)} %copy_bitcast_fusion.1), channel_id=1, source_target_pairs={{0,2},{2,0},{4,6},{6,4},{8,10},{10,8},{12,14},{14,12},{16,18},{18,... | collective-permute-start | bytes 6291464 | tf_op jit(solution)/shard_map/ppermute | solution.py:263
  252.5 40.5 %collective-permute-start.31 = (bf16[512,1024]{1,0:T(8,128)(2,1)S(1)}, bf16[512,1024]{1,0:T(8,128)(2,1)S(1)}, u32[]{:S(2)}, u32[]{:S(2)}) collective-permute-start(bf16[512,1024]{1,0:T(8,128)(2,1)S(1)} %convert_element_type.264), channel_id=1, source_target_pairs={{0,1},{1,0},{2,3},{3,2},{4,5},{5,4},{6,7},{7,6},{8,9},{9,8},{10,11... | collective-permute-start | bytes 3145736 | tf_op jit(solution)/shard_map/ppermute | solution.py:263
  278.4 58.2 %collective-permute-start.50 = (bf16[4,64,2048]{2,1,0:T(8,128)(2,1)}, bf16[4,64,2048]{2,1,0:T(8,128)(2,1)}, u32[]{:S(2)}, u32[]{:S(2)}) collective-permute-start(bf16[4,64,2048]{2,1,0:T(8,128)(2,1)} %fusion.57), channel_id=1, source_target_pairs={{0,4},{2,6},{4,0},{6,2},{8,12},{10,14},{12,8},{14,10},{16,20},{18,... | collective-permute-start | bytes 3145736 | tf_op jit(solution)/shard_map/ppermute | solution.py:263
  281.2 40.8 %collective-permute-start.33 = (bf16[4,64,2048]{2,1,0:T(8,128)(2,1)}, bf16[4,64,2048]{2,1,0:T(8,128)(2,1)}, u32[]{:S(2)}, u32[]{:S(2)}) collective-permute-start(bf16[4,64,2048]{2,1,0:T(8,128)(2,1)} %get-tuple-element.160), channel_id=1, source_target_pairs={{0,4},{2,6},{4,0},{6,2},{8,12},{10,14},{12,8},{14,10},{16,20},{18,... | collective-permute-start | bytes 3145736 | tf_op jit(solution)/shard_map/ppermute | solution.py:263
  316.2 58.3 %collective-permute-start.41 = (bf16[4,2,64,1280]{3,2,0,1:T(8,128)(2,1)}, bf16[4,2,64,1280]{3,2,0,1:T(8,128)(2,1)}, u32[]{:S(2)}, u32[]{:S(2)}) collective-permute-start(bf16[4,2,64,1280]{3,2,0,1:T(8,128)(2,1)} %copy.177), channel_id=1, source_target_pairs={{0,2},{2,0},{4,6},{6,4},{8,10},{10,8},{12,14},{14,12},{16,18},{18,... | collective-permute-start | bytes 3932168 | tf_op jit(solution)/shard_map/ppermute | solution.py:263
  341.2 18.4 %collective-permute-start.51 = (bf16[64,2048]{1,0:T(8,128)(2,1)}, bf16[64,2048]{1,0:T(8,128)(2,1)}, u32[]{:S(2)}, u32[]{:S(2)}) collective-permute-start(bf16[64,2048]{1,0:T(8,128)(2,1)} %get-tuple-element.173), channel_id=1, source_target_pairs={{0,8},{2,10},{4,12},{6,14},{8,16},{10,18},{12,20},{14,22},{16,24},... | collective-permute-start | bytes 786440 | tf_op jit(solution)/shard_map/ppermute | solution.py:268
  341.2 19.1 %collective-permute-start.53 = (bf16[64,2048]{1,0:T(8,128)(2,1)}, bf16[64,2048]{1,0:T(8,128)(2,1)}, u32[]{:S(2)}, u32[]{:S(2)}) collective-permute-start(bf16[64,2048]{1,0:T(8,128)(2,1)} %get-tuple-element.174), channel_id=1, source_target_pairs={{0,24},{2,26},{4,28},{6,30},{8,0},{10,2},{12,4},{14,6},{16,8},{18,... | collective-permute-start | bytes 786440 | tf_op jit(solution)/shard_map/ppermute | solution.py:268
  345.2 26.9 %collective-permute-start.52 = (bf16[64,2048]{1,0:T(8,128)(2,1)}, bf16[64,2048]{1,0:T(8,128)(2,1)}, u32[]{:S(2)}, u32[]{:S(2)}) collective-permute-start(bf16[64,2048]{1,0:T(8,128)(2,1)} %get-tuple-element.175), channel_id=1, source_target_pairs={{0,16},{2,18},{4,20},{6,22},{8,24},{10,26},{12,28},{14,30},{16,0},... | collective-permute-start | bytes 786440 | tf_op jit(solution)/shard_map/ppermute | solution.py:268
  348.7 28.5 %collective-permute-start.34 = (bf16[512,1024]{1,0:T(8,128)(2,1)}, bf16[512,1024]{1,0:T(8,128)(2,1)}, u32[]{:S(2)}, u32[]{:S(2)}) collective-permute-start(bf16[512,1024]{1,0:T(8,128)(2,1)} %get-tuple-element.219), channel_id=1, source_target_pairs={{0,1},{1,0},{2,3},{3,2},{4,5},{5,4},{6,7},{7,6},{8,9},{9,8},{10,11... | collective-permute-start | bytes 3145736 | tf_op jit(solution)/shard_map/ppermute | solution.py:263
  359.5 32.9 %collective-permute-start.46 = (bf16[64,2048]{1,0:T(8,128)(2,1)}, bf16[64,2048]{1,0:T(8,128)(2,1)S(1)}, u32[]{:S(2)}, u32[]{:S(2)}) collective-permute-start(bf16[64,2048]{1,0:T(8,128)(2,1)} %get-tuple-element.176), channel_id=1, source_target_pairs={{0,8},{2,10},{4,12},{6,14},{8,16},{10,18},{12,20},{14,22},{16,24},... | collective-permute-start | bytes 786440 | tf_op jit(solution)/shard_map/ppermute | solution.py:268
  360.2 32.4 %collective-permute-start.48 = (bf16[64,2048]{1,0:T(8,128)(2,1)}, bf16[64,2048]{1,0:T(8,128)(2,1)}, u32[]{:S(2)}, u32[]{:S(2)}) collective-permute-start(bf16[64,2048]{1,0:T(8,128)(2,1)} %get-tuple-element.177), channel_id=1, source_target_pairs={{0,24},{2,26},{4,28},{6,30},{8,0},{10,2},{12,4},{14,6},{16,8},{18,... | collective-permute-start | bytes 786440 | tf_op jit(solution)/shard_map/ppermute | solution.py:268
  372.1 21.9 %collective-permute-start.47 = (bf16[64,2048]{1,0:T(8,128)(2,1)}, bf16[64,2048]{1,0:T(8,128)(2,1)}, u32[]{:S(2)}, u32[]{:S(2)}) collective-permute-start(bf16[64,2048]{1,0:T(8,128)(2,1)} %get-tuple-element.178), channel_id=1, source_target_pairs={{0,16},{2,18},{4,20},{6,22},{8,24},{10,26},{12,28},{14,30},{16,0},... | collective-permute-start | bytes 786440 | tf_op jit(solution)/shard_map/ppermute | solution.py:268
  376.6 10.8 %collective-permute-start.42 = (bf16[4,64,1280]{2,1,0:T(8,128)(2,1)}, bf16[4,64,1280]{2,1,0:T(8,128)(2,1)S(1)}, u32[]{:S(2)}, u32[]{:S(2)}) collective-permute-start(bf16[4,64,1280]{2,1,0:T(8,128)(2,1)} %fusion.85), channel_id=1, source_target_pairs={{0,4},{2,6},{4,0},{6,2},{8,12},{10,14},{12,8},{14,10},{16,20},{18,... | collective-permute-start | bytes 1966088 | tf_op jit(solution)/shard_map/ppermute | solution.py:263
  383.9 12.2 %collective-permute-start.35 = (bf16[4,2,64,896]{3,2,0,1:T(8,128)(2,1)S(1)}, bf16[4,2,64,896]{3,2,0,1:T(8,128)(2,1)S(1)}, u32[]{:S(2)}, u32[]{:S(2)}) collective-permute-start(bf16[4,2,64,896]{3,2,0,1:T(8,128)(2,1)S(1)} %pad_maximum_fusion.9), channel_id=1, source_target_pairs={{0,2},{2,0},{4,6},{6,4},{8,10},{10,8},{12,14},{14,12},{16,18},{18,... | collective-permute-start | bytes 2752520 | tf_op jit(solution)/shard_map/ppermute | solution.py:263
  388.8 8.9 %collective-permute-start.43 = (bf16[64,1280]{1,0:T(8,128)(2,1)S(1)}, bf16[64,1280]{1,0:T(8,128)(2,1)S(1)}, u32[]{:S(2)}, u32[]{:S(2)}) collective-permute-start(bf16[64,1280]{1,0:T(8,128)(2,1)S(1)} %get-tuple-element.189), channel_id=1, source_target_pairs={{0,8},{2,10},{4,12},{6,14},{8,16},{10,18},{12,20},{14,22},{16,24},... | collective-permute-start | bytes 491528 | tf_op jit(solution)/shard_map/ppermute | solution.py:268
  392.6 11.7 %collective-permute-start.44 = (bf16[64,1280]{1,0:T(8,128)(2,1)S(1)}, bf16[64,1280]{1,0:T(8,128)(2,1)S(1)}, u32[]{:S(2)}, u32[]{:S(2)}) collective-permute-start(bf16[64,1280]{1,0:T(8,128)(2,1)S(1)} %get-tuple-element.191), channel_id=1, source_target_pairs={{0,16},{2,18},{4,20},{6,22},{8,24},{10,26},{12,28},{14,30},{16,0},... | collective-permute-start | bytes 491528 | tf_op jit(solution)/shard_map/ppermute | solution.py:268
  396.2 9.1 %collective-permute-start.36 = (bf16[4,64,896]{2,1,0:T(8,128)(2,1)S(1)}, bf16[4,64,896]{2,1,0:T(8,128)(2,1)S(1)}, u32[]{:S(2)}, u32[]{:S(2)}) collective-permute-start(bf16[4,64,896]{2,1,0:T(8,128)(2,1)S(1)} %fusion.99), channel_id=1, source_target_pairs={{0,4},{2,6},{4,0},{6,2},{8,12},{10,14},{12,8},{14,10},{16,20},{18,... | collective-permute-start | bytes 1376264 | tf_op jit(solution)/shard_map/ppermute | solution.py:263
  (62 other events, 539.0 us)
where the time goes:
time: 428 us; the launch traced here: 422 us
  waiting for transfers between devices  145 us (34%)
  matrix products  90.2 us (21%)
  starting transfers between devices  52.7 us (12%)
  Pallas kernels  50.7 us (12%)
  other arithmetic  47.2 us (11%)
  local copies, waits for them, and re-layouts  33.5 us (8%)
    ppermute x30, waiting for transfers between devices, flip(): lax.ppermute(value, axis_name, [(i, i ^ 1 << bit) for i in range(size)])  77 us
    ppermute x24, waiting for transfers between devices, shift(): lax.ppermute(value, axis_name, [(i, (i + amount * step) % size) for i in...  68.3 us
    ppermute x24, starting transfers between devices, shift(): lax.ppermute(value, axis_name, [(i, (i + amount * step) % size) for i in...  33.3 us
    dot_general x10, matrix products, contract_cols(): lax.dot_general(left_rows, right_rows, (((1,), (1,)), ((), ())), preferre...  29.6 us
    dot_general x5, matrix products, contract_rows(): lax.dot_general(left_rows, right_rows, (((0,), (0,)), ((), ())), preferre...  21.5 us
    ppermute x30, starting transfers between devices, flip(): lax.ppermute(value, axis_name, [(i, i ^ 1 << bit) for i in range(size)])  19.4 us
    pallas_call x2, Pallas kernels, attention_back(): pl.pallas_call(functools.partial(attention_back_kernel, tiles=tiles, bloc...  18.7 us
    pallas_call x4, Pallas kernels, place_blocks(): out = out(where, *pieces)  17.6 us
  transfers between devices with their start and end apart: 54, of which 22 were waited for; matrix products, arithmetic and copies ran while one was open for 29% of the time, Pallas kernels for 12%

commit v1 on v0

--- a/solution.py
+++ b/solution.py
@@ -254,6 +254,9 @@
     )(lengths, projected, mixed, grad_mixed, log_sums)
 
 
+DP, TP = "dp", "tensor"
+
+
 def tie(*values):
     return lax.optimization_barrier(values)
 
@@ -301,16 +304,16 @@
 
 
 def gather_line(block):
-    line = lax.axis_size("dp") // 4
-    return [block] + [shift(block, "dp", 4, k) for k in range(1, line)]
+    line = lax.axis_size(DP) // 4
+    return [block] + [shift(block, DP, 4, k) for k in range(1, line)]
 
 
 def gather_rest(blocks):
     line = len(blocks)
     own = jnp.stack(blocks)
-    side = flip(own, "dp", 1)
-    index = lax.axis_index("dp")
-    pieces = [own, side] + [flip(half, "dp", 0) for half in (own, side)]
+    side = flip(own, DP, 1)
+    index = lax.axis_index(DP)
+    pieces = [own, side] + [flip(half, DP, 0) for half in (own, side)]
     back = (index // 4 - jnp.arange(line)) % line
     where = jnp.concatenate([back * 4 + ((index % 4) ^ mask) for mask in (0, 2, 1, 3)])
     return place_blocks(pieces, where.astype(jnp.int32))
@@ -321,8 +324,8 @@
 
 
 def scatter_core(wholes):
-    size = lax.axis_size("dp")
-    core = lax.axis_index("dp") % 2
+    size = lax.axis_size(DP)
+    core, *wholes = tie(lax.axis_index(DP) % 2, *wholes)
     blocks = [
         whole.reshape(size // 4, 2, 2, whole.shape[0] // size, whole.shape[1]) for whole in wholes
     ]
@@ -330,25 +333,26 @@
     def taken(at):
         return jnp.concatenate([pick(block, at, 2) for block in blocks], axis=-1)
 
-    return taken(core), flip(taken(1 - core), "dp", 0)
+    return taken(core), flip(taken(1 - core), DP, 0)
 
 
 def scatter_side(kept, met):
-    side = (lax.axis_index("dp") // 2) % 2
+    side = (lax.axis_index(DP) // 2) % 2
 
     def summed(at):
         return pick(kept, at, 1).astype(jnp.float32) + pick(met, at, 1).astype(jnp.float32)
 
-    return summed(side), flip(summed(1 - side).astype(jnp.bfloat16), "dp", 1)
+    sent = summed(1 - side).astype(jnp.bfloat16)
+    return summed(side), flip(sent, DP, 1)
 
 
 def scatter_line(mine, crossed):
     line = mine.shape[0]
-    at = lax.axis_index("dp") // 4
+    at = lax.axis_index(DP) // 4
     sums = mine + crossed.astype(jnp.float32)
     low = sums.astype(jnp.bfloat16)
     return [pick(sums, at, 0)] + [
-        shift(pick(low, (at + k) % line, 0), "dp", 4, k) for k in range(1, line)
+        shift(pick(low, (at + k) % line, 0), DP, 4, k) for k in range(1, line)
     ]
 
 
@@ -363,26 +367,26 @@
 
 
 def relative(whole):
-    size = lax.axis_size("tensor")
+    size = lax.axis_size(TP)
     blocks = whole.reshape((size, whole.shape[0] // size) + whole.shape[1:])
-    return [pick(blocks, lax.axis_index("tensor") ^ j, 0) for j in range(size)]
+    return [pick(blocks, lax.axis_index(TP) ^ j, 0) for j in range(size)]
 
 
 def gather_tensor(block):
     current = block
-    for bit in range(bits_of(lax.axis_size("tensor"))):
-        current = jnp.concatenate([current, flip(current, "tensor", bit)])
+    for bit in range(bits_of(lax.axis_size(TP))):
+        current = jnp.concatenate([current, flip(current, TP, bit)])
     return current[block.shape[0] :]
 
 
 def scatter_tensor(own, rest):
     rows = own.shape[0]
     blocks = [own] + [rest[at : at + rows] for at in range(0, rest.shape[0], rows)]
-    for bit in reversed(range(bits_of(lax.axis_size("tensor")))):
+    for bit in reversed(range(bits_of(lax.axis_size(TP)))):
         half = len(blocks) // 2
         sent = blocks[half:]
         sent = sent[0] if half == 1 else jnp.concatenate(sent)
-        met = flip(sent.astype(jnp.bfloat16), "tensor", bit)
+        met = flip(sent.astype(jnp.bfloat16), TP, bit)
         blocks = [
             block + met[j * rows : (j + 1) * rows].astype(jnp.float32)
             for j, block in enumerate(blocks[:half])
@@ -419,8 +423,8 @@
     down_weight,
     down_bias,
 ):
-    dp, tp = lax.axis_size("dp"), lax.axis_size("tensor")
-    local_rows, model_width = tokens.shape
+    dp = lax.axis_size(DP)
+    _, model_width = tokens.shape
     shard_rows = model_width // dp
     head_local = qkv_bias.shape[1]
     head_width = qkv_bias.shape[2] * dp
@@ -447,16 +451,11 @@
     shard_list = [jnp.concatenate(piece, axis=1) for piece in columns]
     up_shard, down_shard = up_weight, down_weight.T
 
-    half = local_rows // 2
-    rest_rows = [gather_tensor(tokens[:half])]
+    tokens_rest = gather_tensor(tokens)
     lines = [gather_line(shard_list[0])]
-    late_tokens, _ = tie(tokens[half:], rest_rows[0])
     for piece in shard_list[1:]:
-        piece, *_ = tie(piece, rest_rows[0], *lines[-1])
+        piece, *_ = tie(piece, *lines[-1])
         lines.append(gather_line(piece))
-    rest_rows.append(gather_tensor(late_tokens))
-    others = [part.reshape(tp - 1, half, model_width) for part in rest_rows]
-    tokens_rest = jnp.concatenate(others, axis=1).reshape((tp - 1) * local_rows, model_width)
     cotangent_late, tokens_rest = tie(cotangent, tokens_rest)
     cotangent_rest = gather_tensor(cotangent_late)
 
@@ -548,12 +547,13 @@
     down_core = scatter_core([grad_down])
     up_core = scatter_core([grad_up])
     grad_down_bias = jnp.sum(cotangent.astype(jnp.float32), axis=0)
-    grad_ln2_gain = jnp.sum(grad_norm2 * scaled2, axis=0)
-    grad_ln2_bias = jnp.sum(grad_norm2, axis=0)
     grad_middle = cotangent.astype(jnp.float32) + normalize_back(
         grad_norm2, scaled2, inverse2, norm2_gain
     )
-    grad_out_bias = jnp.sum(grad_middle, axis=0)
+    seen = tie(grad_norm2, scaled2, grad_middle)
+    grad_ln2_gain = jnp.sum(seen[0] * seen[1], axis=0)
+    grad_ln2_bias = jnp.sum(seen[0], axis=0)
+    grad_out_bias = jnp.sum(seen[2], axis=0)
     grad_middle_own = grad_middle.astype(jnp.bfloat16)
     grad_middle_rest = gather_tensor(grad_middle_own)
     down_side = scatter_side(*down_core)
@@ -570,12 +570,9 @@
     width = local_width // parts
     grad_parts, bias_parts = [], []
     down_own = scatter_line(*down_side)
-    up_own = None
+    up_own = scatter_line(*up_side)
     for part in range(parts):
         upstream = grad_mixed[:, part * width : (part + 1) * width]
-        if part == parts - 1:
-            upstream, *up_side = tie(upstream, *up_side)
-            up_own = scatter_line(*up_side)
         grads, bias_sums = attention_back(
             lengths, projected[part], attended[part][0], upstream, attended[part][1], head_width
         )
@@ -593,9 +590,9 @@
     part_rest = first_grad([jnp.concatenate(blocks[1:]) for blocks in by_owner])
     (part_own,) = tie(first_grad([blocks[0] for blocks in by_owner]))
     grad_norm1 = scatter_tensor(part_own, part_rest)
-    seen_own, seen_rest = tie(part_own, part_rest)
+    seen_own, seen_rest, seen_scaled = tie(part_own, part_rest, scaled1)
     grad_ln1_gain, grad_ln1_bias = tie(
-        jnp.sum(seen_own * scaled1, axis=0) + jnp.sum(seen_rest * scaled1_rest, axis=0),
+        jnp.sum(seen_own * seen_scaled, axis=0) + jnp.sum(seen_rest * scaled1_rest, axis=0),
         jnp.sum(seen_own, axis=0) + jnp.sum(seen_rest, axis=0),
     )
     grad_qkv = []
@@ -633,6 +630,7 @@
         core = scatter_core(piece)
         own.append(total_of(scatter_line(*scatter_side(*core))))
     up_shard, down_shard = total_of(up_own), total_of(down_own)
+    down_final = down_shard.T
     out_shard = own[0][:, part_cols : part_cols + local_width]
     sums_own = own[-1][:, -small_width:].T[:up_end]
     qkv_shard = (
@@ -641,7 +639,7 @@
         .transpose(0, 2, 1, 3)
         .reshape(shard_rows, 3, local_width)
     )
-    vector_sums = sum_over(sums_own[:6], "tensor")
+    vector_sums = sum_over(sums_own[:6], TP)
     grad_tokens = grad_middle + normalize_back(grad_norm1, scaled1, inverse1, norm1_gain)
     return (
         output,
@@ -656,43 +654,43 @@
         vector_sums[4],
         up_shard,
         sums_own[up_at:up_end].reshape(-1)[: up_bias.size].reshape(up_bias.shape),
-        down_shard.T,
+        down_final,
         vector_sums[5],
     )
 
 
 def solution(mesh):
     in_specs = (
-        P(("dp", "tensor"), None),
-        P(("dp", "tensor"), None),
-        P("dp", None),
-        P("dp"),
-        P("dp"),
-        P("dp", None, "tensor"),
-        P(None, "tensor", "dp"),
-        P("tensor", "dp"),
-        P("dp"),
-        P("dp"),
-        P("dp"),
-        P("dp", "tensor"),
-        P("tensor", "dp"),
-        P("tensor", "dp"),
-        P("dp"),
+        P((DP, TP), None),
+        P((DP, TP), None),
+        P(DP, None),
+        P(DP),
+        P(DP),
+        P(DP, None, TP),
+        P(None, TP, DP),
+        P(TP, DP),
+        P(DP),
+        P(DP),
+        P(DP),
+        P(DP, TP),
+        P(TP, DP),
+        P(TP, DP),
+        P(DP),
     )
     out_specs = (
-        P(("dp", "tensor"), None),
-        P(("dp", "tensor"), None),
-        P("dp"),
-        P("dp"),
-        P("dp", None, "tensor"),
-        P(None, "tensor", "dp"),
-        P("tensor", "dp"),
-        P("dp"),
-        P("dp"),
-        P("dp"),
-        P("dp", "tensor"),
-        P("tensor", "dp"),
-        P("tensor", "dp"),
-        P("dp"),
+        P((DP, TP), None),
+        P((DP, TP), None),
+        P(DP),
+        P(DP),
+        P(DP, None, TP),
+        P(None, TP, DP),
+        P(TP, DP),
+        P(DP),
+        P(DP),
+        P(DP),
+        P(DP, TP),
+        P(TP, DP),
+        P(TP, DP),
+        P(DP),
     )
     return jax.shard_map(block, mesh=mesh, in_specs=in_specs, out_specs=out_specs, check_vma=False)

time: 428 us -> 473 us (1.11)
  waiting for transfers between devices: 145 us -> 168 us
  local copies, waits for them, and re-layouts: 33.5 us -> 43.7 us
  starting transfers between devices: 52.7 us -> 58.1 us
    ppermute x24, waiting for transfers between devices: 68.3 us -> 86.5 us  [shift(): lax.ppermute(value, axis_name, [(i, (i + amount * step) % size) for i in...]
    unnamed x119 -> x135, local copies, waits for them, and re-layouts: 9.84 us -> 17.5 us
    squeeze x12, local copies, waits for them, and re-layouts: 6.05 us -> 11.8 us  [pick(): return lax.dynamic_index_in_dim(values, at, axis, keepdims=False)]
    dot_general x10, matrix products: 29.6 us -> 35.2 us  [contract_cols(): lax.dot_general(left_rows, right_rows, (((1,), (1,)), ((), ())), preferre...]
    dot_general x2, matrix products: 12.1 us -> 7.25 us  [feed_forward(): jnp.dot(normed, up_full, preferred_element_type=jnp.float32) + up_shift]
    ppermute x30 -> x29, waiting for transfers between devices: 77 us -> 81.1 us  [flip(): lax.ppermute(value, axis_name, [(i, i ^ 1 << bit) for i in range(size)])]
    ppermute x30 -> x29, starting transfers between devices: 19.4 us -> 20.6 us  [flip(): lax.ppermute(value, axis_name, [(i, i ^ 1 << bit) for i in range(size)])]
  transfers between devices with their start and end apart: 54 -> 53, of which waited for: 22 -> 22; matrix products, arithmetic and copies ran while one was open for 29% -> 27% of each run, Pallas kernels for 12% -> 11%
where the time goes in v1:
time: 473 us; the launch traced here: 465 us
  waiting for transfers between devices  168 us (36%)
  matrix products  91.6 us (19%)
  starting transfers between devices  58.1 us (12%)
  other arithmetic  51.6 us (11%)
  Pallas kernels  50.3 us (11%)
  local copies, waits for them, and re-layouts  43.7 us (9%)
    ppermute x24, waiting for transfers between devices, shift(): lax.ppermute(value, axis_name, [(i, (i + amount * step) % size) for i in...  86.5 us
    ppermute x29, waiting for transfers between devices, flip(): lax.ppermute(value, axis_name, [(i, i ^ 1 << bit) for i in range(size)])  81.1 us
    ppermute x24, starting transfers between devices, shift(): lax.ppermute(value, axis_name, [(i, (i + amount * step) % size) for i in...  37.5 us
    dot_general x10, matrix products, contract_cols(): lax.dot_general(left_rows, right_rows, (((1,), (1,)), ((), ())), preferre...  35.2 us
    dot_general x5, matrix products, contract_rows(): lax.dot_general(left_rows, right_rows, (((0,), (0,)), ((), ())), preferre...  25.6 us
    ppermute x29, starting transfers between devices, flip(): lax.ppermute(value, axis_name, [(i, i ^ 1 << bit) for i in range(size)])  20.6 us
    pallas_call x2, Pallas kernels, attention_back(): pl.pallas_call(functools.partial(attention_back_kernel, tiles=tiles, bloc...  18.5 us
    pallas_call x4, Pallas kernels, place_blocks(): out = out(where, *pieces)  17.5 us
  transfers between devices with their start and end apart: 53, of which 22 were waited for; matrix products, arithmetic and copies ran while one was open for 27% of the time, Pallas kernels for 11%

profile of v1, /device:TPU:0, one launch (start us, length us, event | category | flops | bytes accessed | tf_op | source)
XLA Modules:
  0.0 465.3 jit_solution(2697536173051340059)
XLA Ops:
  5.2 5.1 %collective-permute-start.2 = (bf16[64,896]{1,0:T(8,128)(2,1)S(1)}, bf16[64,896]{1,0:T(8,128)(2,1)S(1)}, u32[]{:S(2)}, u32[]{:S(2)}) collective-permute-start(bf16[64,896]{1,0:T(8,128)(2,1)S(1)} %get-tuple-element.229), channel_id=1, source_target_pairs={{0,24},{2,26},{4,28},{6,30},{8,0},{10,2},{12,4},{14,6},{16,8},{18,... | collective-permute-start | bytes 344072 | tf_op jit(solution)/shard_map/ppermute | solution.py:271
  13.8 6.5 %collective-permute-done.1 = bf16[64,896]{1,0:T(8,128)(2,1)S(1)} collective-permute-done((bf16[64,896]{1,0:T(8,128)(2,1)S(1)}, bf16[64,896]{1,0:T(8,128)(2,1)S(1)}, u32[]{:S(2)}, u32[]{:S(2)}) %collective-permute-start.1) | collective-permute-done | bytes 114720 | tf_op jit(solution)/shard_map/ppermute | solution.py:271
  26.6 10.3 %collective-permute-done.8 = bf16[64,1280]{1,0:T(8,128)(2,1)S(1)} collective-permute-done((bf16[64,1280]{1,0:T(8,128)(2,1)S(1)}, bf16[64,1280]{1,0:T(8,128)(2,1)S(1)}, u32[]{:S(2)}, u32[]{:S(2)}) %collective-permute-start.8) | collective-permute-done | bytes 163872 | tf_op jit(solution)/shard_map/ppermute | solution.py:271
  41.6 3.5 collective-permute-done.17
  45.1 16.1 %collective-permute-done.16 = bf16[64,2048]{1,0:T(8,128)(2,1)S(1)} collective-permute-done((bf16[64,2048]{1,0:T(8,128)(2,1)S(1)}, bf16[64,2048]{1,0:T(8,128)(2,1)S(1)}, u32[]{:S(2)}, u32[]{:S(2)}) %collective-permute-start.16) | collective-permute-done | bytes 262176 | tf_op jit(solution)/shard_map/ppermute | solution.py:271
  71.9 14.4 %collective-permute-done.22 = bf16[64,2048]{1,0:T(8,128)(2,1)} collective-permute-done((bf16[64,2048]{1,0:T(8,128)(2,1)}, bf16[64,2048]{1,0:T(8,128)(2,1)}, u32[]{:S(2)}, u32[]{:S(2)}) %collective-permute-start.22) | collective-permute-done | bytes 262176 | tf_op jit(solution)/shard_map/ppermute | solution.py:271
  93.1 3.6 place_blocks.4
  101.0 9.8 %collective-permute-done.6 = bf16[512,1024]{1,0:T(8,128)(2,1)S(1)} collective-permute-done((bf16[512,1024]{1,0:T(8,128)(2,1)S(1)}, bf16[512,1024]{1,0:T(8,128)(2,1)S(1)}, u32[]{:S(2)}, u32[]{:S(2)}) %collective-permute-start.6) | collective-permute-done | bytes 1048608 | tf_op jit(solution)/shard_map/ppermute | solution.py:266
  120.7 7.3 %attention.2 = (bf16[1024,256]{1,0:T(8,128)(2,1)}, f32[16,1024]{1,0:T(8,128)}) custom-call(s32[1,8]{1,0:T(1,128)} %lengths_ref.7, bf16[1024,768]{1,0:T(8,128)(2,1)} %add_convert_fusion.1.x_ref), custom_call_target="tpu_custom_call" | custom-call | tf_op jit(solution)/shard_map/attention/pallas_call | solution.py:195
  128.6 4.0 place_blocks.5
  132.6 4.8 %add_convert_fusion.x_ref = bf16[1024,768]{1,0:T(8,128)(2,1)} fusion(f32[768]{0:T(1024)S(1)} %add.537, bf16[1024,1280]{1,0:T(8,128)(2,1)} %bitcast.285, bf16[512,1024]{1,0:T(8,128)(2,1)} %copy-done.39, bf16[512,1024]{1,0:T(8,128)(2,1)S(1)} %get-tuple-element.187), kind=kOutput, calls=%fused_computation.30 | convolution fusion | flops 1616379904 | bytes 5245952 | tf_op jit(solution)/shard_map/dot_general | solution.py:495
  138.7 7.1 %attention.3 = (bf16[1024,256]{1,0:T(8,128)(2,1)}, f32[16,1024]{1,0:T(8,128)}) custom-call(s32[1,8]{1,0:T(1,128)} %lengths_ref.7, bf16[1024,768]{1,0:T(8,128)(2,1)} %add_convert_fusion.x_ref), custom_call_target="tpu_custom_call" | custom-call | tf_op jit(solution)/shard_map/attention/pallas_call | solution.py:195
  155.8 4.9 %place_blocks.6 = bf16[16,64,2048]{2,1,0:T(8,128)(2,1)} custom-call(s32[16]{0:T(128)} %pad_add_fusion.where_ref, bf16[4,64,2048]{2,1,0:T(8,128)(2,1)} %pad_maximum_fusion.7.refs_0_, bf16[4,64,2048]{2,1,0:T(8,128)(2,1)} %collective-permute-done.18.refs_1_, bf16[4,64,2048]{2,1,0:T(8,128)(2,1)} %collective-permute-done.19.refs_2_, ...), custom_call_target="tpu_custom_call" | custom-call | tf_op jit(solution)/shard_map/place_blocks/pallas_call | solution.py:302
  160.8 4.9 %place_blocks.7 = bf16[16,64,2048]{2,1,0:T(8,128)(2,1)} custom-call(s32[16]{0:T(128)} %pad_add_fusion.where_ref, bf16[4,64,2048]{2,1,0:T(8,128)(2,1)} %pad_maximum_fusion.8.refs_0_, bf16[4,64,2048]{2,1,0:T(8,128)(2,1)} %collective-permute-done.24.refs_1_, bf16[4,64,2048]{2,1,0:T(8,128)(2,1)} %collective-permute-done.25.refs_2_, ...), custom_call_target="tpu_custom_call" | custom-call | tf_op jit(solution)/shard_map/place_blocks/pallas_call | solution.py:302
  165.7 11.7 %collective-permute-done.14 = bf16[512,1024]{1,0:T(8,128)(2,1)} collective-permute-done((bf16[512,1024]{1,0:T(8,128)(2,1)}, bf16[512,1024]{1,0:T(8,128)(2,1)}, u32[]{:S(2)}, u32[]{:S(2)}) %collective-permute-start.14) | collective-permute-done | bytes 1048608 | tf_op jit(solution)/shard_map/ppermute | solution.py:266
  185.7 6.1 %fusion.118 = (f32[2048]{0:T(1024)S(1)}, bf16[512,2048]{1,0:T(8,128)(2,1)}) fusion(f32[512,2048]{1,0:T(8,128)S(1)} %fusion.124, f32[2048]{0:T(1024)S(1)} %add.549, bf16[512,1024]{1,0:T(8,128)(2,1)S(1)} %copy-done.23, bf16[1024,2048]{1,0:T(8,128)(2,1)S(1)} %bitcast.292), kind=kOutput, calls=%fused_computation.255 | convolution fusion | flops 2169501696 | bytes 11550720 | tf_op jit(solution)/shard_map/dot_general | solution.py:531
  191.7 13.4 %collective-permute-done.27 = bf16[512,1024]{1,0:T(8,128)(2,1)S(1)} collective-permute-done((bf16[512,1024]{1,0:T(8,128)(2,1)S(1)}, bf16[512,1024]{1,0:T(8,128)(2,1)S(1)}, u32[]{:S(2)}, u32[]{:S(2)}) %collective-permute-start.27) | collective-permute-done | bytes 1048608 | tf_op jit(solution)/shard_map/ppermute | solution.py:266
  205.1 4.9 %multiply_convert_fusion = (bf16[512,2048]{1,0:T(8,128)(2,1)S(1)}, bf16[512,2048]{1,0:T(8,128)(2,1)S(1)}, f32[512,2048]{1,0:T(8,128)S(1)}) fusion(f32[2048]{0:T(1024)S(1)} %add.549, f32[512,2048]{1,0:T(8,128)S(1)} %fusion.124, bf16[512,1024]{1,0:T(8,128)(2,1)S(1)} %collective-permute-done.27, bf16[1024,2048]{1,0:T(8,128)(2,1)S(1)} %bitcast.297), kind=kOutput, calls=%fused_computation.26 | convolution fusion | flops 2168455168 | bytes 17833984 | tf_op jit(solution)/shard_map/dot_general | solution.py:530
  210.1 3.7 fusion.125
  213.7 6.9 %fusion.117 = (f32[2048]{0:T(1024)S(1)}, bf16[512,2048]{1,0:T(8,128)(2,1)}) fusion(f32[512,2048]{1,0:T(8,128)S(1)} %get-tuple-element.235, f32[2048]{0:T(1024)S(1)} %add.549, bf16[512,1024]{1,0:T(8,128)(2,1)} %collective-permute-done.13, bf16[1024,2048]{1,0:T(8,128)(2,1)S(1)} %bitcast.294), kind=kOutput, calls=%fused_computation.254 | convolution fusion | flops 2169501696 | bytes 11550720 | tf_op jit(solution)/shard_map/dot_general | solution.py:531
  220.7 7.5 %fusion.22 = bf16[1024,2048]{1,0:T(8,128)(2,1)} fusion(bf16[512,2048]{1,0:T(8,128)(2,1)S(1)} %get-tuple-element.65, bf16[512,2048]{1,0:T(8,128)(2,1)S(1)} %get-tuple-element.63, bf16[512,1024]{1,0:T(8,128)(2,1)} %collective-permute-done.13, bf16[512,1024]{1,0:T(8,128)(2,1)S(1)} %copy-done.23), kind=kOutput, calls=%fused_computation.28 | convolution fusion | flops 4309647360 | bytes 10485760 | tf_op jit(solution)/shard_map/dot_general | solution.py:48
  228.1 6.4 %convolution_convert_fusion.5 = bf16[512,1024]{1,0:T(8,128)(2,1)} fusion(bf16[512,2048]{1,0:T(8,128)(2,1)} %get-tuple-element.69, bf16[1024,2048]{1,0:T(8,128)(2,1)} %bitcast.295), kind=kOutput, calls=%fused_computation.92 | convolution fusion | flops 2148007936 | bytes 7340032 | tf_op jit(solution)/shard_map/dot_general | solution.py:54
  234.5 3.7 fusion.126
  238.3 6.5 %fusion.25 = bf16[1024,2048]{1,0:T(8,128)(2,1)} fusion(bf16[512,2048]{1,0:T(8,128)(2,1)S(1)} %copy-done.63, bf16[512,2048]{1,0:T(8,128)(2,1)S(1)} %copy-done.61, bf16[512,1024]{1,0:T(8,128)(2,1)S(1)} %copy-done.60, bf16[512,1024]{1,0:T(8,128)(2,1)S(1)} %copy-done.44), kind=kOutput, calls=%fused_computation.29 | convolution fusion | flops 4309647360 | bytes 10485760 | tf_op jit(solution)/shard_map/dot_general | solution.py:48
  246.1 6.2 %convolution_convert_fusion.6 = bf16[512,1024]{1,0:T(8,128)(2,1)} fusion(bf16[512,2048]{1,0:T(8,128)(2,1)} %copy-done.62, bf16[1024,2048]{1,0:T(8,128)(2,1)} %bitcast.291), kind=kOutput, calls=%fused_computation.93 | convolution fusion | flops 2148007936 | bytes 7340032 | tf_op jit(solution)/shard_map/dot_general | solution.py:54
  253.7 3.2 copy_bitcast_fusion
  256.9 3.3 copy_bitcast_fusion.1
  260.7 11.1 %collective-permute-done.29 = bf16[512,1024]{1,0:T(8,128)(2,1)} collective-permute-done((bf16[512,1024]{1,0:T(8,128)(2,1)}, bf16[512,1024]{1,0:T(8,128)(2,1)}, u32[]{:S(2)}, u32[]{:S(2)}) %collective-permute-start.29) | collective-permute-done | bytes 1048608 | tf_op jit(solution)/shard_map/ppermute | solution.py:266
  276.8 17.5 %collective-permute-done.28 = bf16[512,1024]{1,0:T(8,128)(2,1)} collective-permute-done((bf16[512,1024]{1,0:T(8,128)(2,1)}, bf16[512,1024]{1,0:T(8,128)(2,1)}, u32[]{:S(2)}, u32[]{:S(2)}) %collective-permute-start.28) | collective-permute-done | bytes 1048608 | tf_op jit(solution)/shard_map/ppermute | solution.py:266
  299.5 3.4 add_add_fusion
  311.1 3.5 collective-permute-done.30
  318.6 9.3 %attention_back.3 = (bf16[1024,768]{1,0:T(8,128)(2,1)}, f32[8,256]{1,0:T(8,128)}) custom-call(s32[1,8]{1,0:T(1,128)} %lengths_ref.7, bf16[1024,768]{1,0:T(8,128)(2,1)} %add_convert_fusion.x_ref, bf16[1024,256]{1,0:T(8,128)(2,1)} %get-tuple-element.60.o_ref, bf16[1024,256]{1,0:T(8,128)(2,1)} %get-tuple-element.204.do_ref, f32[16,1024]{1,0:T(8,128)} %get-tuple-element.72.lse_ref), custom_call_target="tpu_custom_call" | custom-call | tf_op jit(solution)/shard_map/attention_back/pallas_call | solution.py:226
  328.0 4.5 convolution_convert_fusion.1
  337.2 9.2 %attention_back.2 = (bf16[1024,768]{1,0:T(8,128)(2,1)}, f32[8,256]{1,0:T(8,128)}) custom-call(s32[1,8]{1,0:T(1,128)} %lengths_ref.7, bf16[1024,768]{1,0:T(8,128)(2,1)} %add_convert_fusion.1.x_ref, bf16[1024,256]{1,0:T(8,128)(2,1)} %get-tuple-element.56.o_ref, bf16[1024,256]{1,0:T(8,128)(2,1)} %get-tuple-element.203.do_ref, f32[16,1024]{1,0:T(8,128)} %get-tuple-element.70.lse_ref), custom_call_target="tpu_custom_call" | custom-call | tf_op jit(solution)/shard_map/attention_back/pallas_call | solution.py:226
  348.1 3.5 convolution_add_fusion.1
  363.6 4.0 convolution_convert_fusion.2
  367.6 3.1 convolution_convert_fusion
  380.0 3.8 collective-permute-start.52
  386.3 12.7 %collective-permute-done.31 = bf16[512,1024]{1,0:T(8,128)(2,1)S(1)} collective-permute-done((bf16[512,1024]{1,0:T(8,128)(2,1)S(1)}, bf16[512,1024]{1,0:T(8,128)(2,1)S(1)}, u32[]{:S(2)}, u32[]{:S(2)}) %collective-permute-start.31) | collective-permute-done | bytes 1048608 | tf_op jit(solution)/shard_map/ppermute | solution.py:266
  402.7 3.8 collective-permute-start.47
  406.5 9.0 %collective-permute-done.51 = bf16[64,2048]{1,0:T(8,128)(2,1)S(1)} collective-permute-done((bf16[64,2048]{1,0:T(8,128)(2,1)S(1)}, bf16[64,2048]{1,0:T(8,128)(2,1)S(1)}, u32[]{:S(2)}, u32[]{:S(2)}) %collective-permute-start.51) | collective-permute-done | bytes 262176 | tf_op jit(solution)/shard_map/ppermute | solution.py:271
  420.4 3.8 collective-permute-start.36
  424.3 5.8 %collective-permute-start.35 = (bf16[64,896]{1,0:T(8,128)(2,1)S(1)}, bf16[64,896]{1,0:T(8,128)(2,1)S(1)}, u32[]{:S(2)}, u32[]{:S(2)}) collective-permute-start(bf16[64,896]{1,0:T(8,128)(2,1)S(1)} %get-tuple-element.221), channel_id=1, source_target_pairs={{0,16},{2,18},{4,20},{6,22},{8,24},{10,26},{12,28},{14,30},{16,0},... | collective-permute-start | bytes 344072 | tf_op jit(solution)/shard_map/ppermute | solution.py:271
  430.0 7.3 %collective-permute-done.46 = bf16[64,2048]{1,0:T(8,128)(2,1)S(1)} collective-permute-done((bf16[64,2048]{1,0:T(8,128)(2,1)S(1)}, bf16[64,2048]{1,0:T(8,128)(2,1)S(1)}, u32[]{:S(2)}, u32[]{:S(2)}) %collective-permute-start.46) | collective-permute-done | bytes 262176 | tf_op jit(solution)/shard_map/ppermute | solution.py:271
  438.2 3.9 collective-permute-done.35
  447.1 3.8 collective-permute-start.42
  451.8 4.2 collective-permute-done.40
  458.7 4.0 collective-permute-done.41
  (361 shorter events, 146.0 us)
Async XLA Ops:
  10.3 10.0 %collective-permute-start.1 = (bf16[64,896]{1,0:T(8,128)(2,1)S(1)}, bf16[64,896]{1,0:T(8,128)(2,1)S(1)}, u32[]{:S(2)}, u32[]{:S(2)}) collective-permute-start(bf16[64,896]{1,0:T(8,128)(2,1)S(1)} %get-tuple-element.229), channel_id=1, source_target_pairs={{0,16},{2,18},{4,20},{6,22},{8,24},{10,26},{12,28},{14,30},{16,0},... | collective-permute-start | bytes 344072 | tf_op jit(solution)/shard_map/ppermute | solution.py:271
  10.3 10.0 %collective-permute-start = (bf16[64,896]{1,0:T(8,128)(2,1)S(1)}, bf16[64,896]{1,0:T(8,128)(2,1)S(1)}, u32[]{:S(2)}, u32[]{:S(2)}) collective-permute-start(bf16[64,896]{1,0:T(8,128)(2,1)S(1)} %get-tuple-element.229), channel_id=1, source_target_pairs={{0,8},{2,10},{4,12},{6,14},{8,16},{10,18},{12,20},{14,22},{16,24},... | collective-permute-start | bytes 344072 | tf_op jit(solution)/shard_map/ppermute | solution.py:271
  22.0 14.9 %collective-permute-start.8 = (bf16[64,1280]{1,0:T(8,128)(2,1)S(1)}, bf16[64,1280]{1,0:T(8,128)(2,1)S(1)}, u32[]{:S(2)}, u32[]{:S(2)}) collective-permute-start(bf16[64,1280]{1,0:T(8,128)(2,1)S(1)} %pad_maximum_fusion.14), channel_id=1, source_target_pairs={{0,16},{2,18},{4,20},{6,22},{8,24},{10,26},{12,28},{14,30},{16,0},... | collective-permute-start | bytes 491528 | tf_op jit(solution)/shard_map/ppermute | solution.py:271
  22.7 14.8 %collective-permute-start.7 = (bf16[64,1280]{1,0:T(8,128)(2,1)S(1)}, bf16[64,1280]{1,0:T(8,128)(2,1)S(1)}, u32[]{:S(2)}, u32[]{:S(2)}) collective-permute-start(bf16[64,1280]{1,0:T(8,128)(2,1)S(1)} %pad_maximum_fusion.14), channel_id=1, source_target_pairs={{0,8},{2,10},{4,12},{6,14},{8,16},{10,18},{12,20},{14,22},{16,24},... | collective-permute-start | bytes 491528 | tf_op jit(solution)/shard_map/ppermute | solution.py:271
  37.6 23.6 %collective-permute-start.16 = (bf16[64,2048]{1,0:T(8,128)(2,1)S(1)}, bf16[64,2048]{1,0:T(8,128)(2,1)S(1)}, u32[]{:S(2)}, u32[]{:S(2)}) collective-permute-start(bf16[64,2048]{1,0:T(8,128)(2,1)S(1)} %copy-done.52), channel_id=1, source_target_pairs={{0,16},{2,18},{4,20},{6,22},{8,24},{10,26},{12,28},{14,30},{16,0},... | collective-permute-start | bytes 786440 | tf_op jit(solution)/shard_map/ppermute | solution.py:271
  38.0 23.3 %collective-permute-start.15 = (bf16[64,2048]{1,0:T(8,128)(2,1)S(1)}, bf16[64,2048]{1,0:T(8,128)(2,1)S(1)}, u32[]{:S(2)}, u32[]{:S(2)}) collective-permute-start(bf16[64,2048]{1,0:T(8,128)(2,1)S(1)} %copy-done.52), channel_id=1, source_target_pairs={{0,8},{2,10},{4,12},{6,14},{8,16},{10,18},{12,20},{14,22},{16,24},... | collective-permute-start | bytes 786440 | tf_op jit(solution)/shard_map/ppermute | solution.py:271
  40.1 28.7 %collective-permute-start.3 = (bf16[4,64,896]{2,1,0:T(8,128)(2,1)S(1)}, bf16[4,64,896]{2,1,0:T(8,128)(2,1)S(1)}, u32[]{:S(2)}, u32[]{:S(2)}) collective-permute-start(bf16[4,64,896]{2,1,0:T(8,128)(2,1)S(1)} %pad_maximum_fusion.12.refs_0_), channel_id=1, source_target_pairs={{0,4},{2,6},{4,0},{6,2},{8,12},{10,14},{12,8},{14,10},{16,20},{18,... | collective-permute-start | bytes 1376264 | tf_op jit(solution)/shard_map/ppermute | solution.py:266
  63.4 28.4 %collective-permute-start.10 = (bf16[4,64,1280]{2,1,0:T(8,128)(2,1)}, bf16[4,64,1280]{2,1,0:T(8,128)(2,1)}, u32[]{:S(2)}, u32[]{:S(2)}) collective-permute-start(bf16[4,64,1280]{2,1,0:T(8,128)(2,1)} %pad_maximum_fusion.10.refs_0_), channel_id=1, source_target_pairs={{0,4},{2,6},{4,0},{6,2},{8,12},{10,14},{12,8},{14,10},{16,20},{18,... | collective-permute-start | bytes 1966088 | tf_op jit(solution)/shard_map/ppermute | solution.py:266
  64.9 21.4 %collective-permute-start.22 = (bf16[64,2048]{1,0:T(8,128)(2,1)}, bf16[64,2048]{1,0:T(8,128)(2,1)}, u32[]{:S(2)}, u32[]{:S(2)}) collective-permute-start(bf16[64,2048]{1,0:T(8,128)(2,1)} %bitcast.42), channel_id=1, source_target_pairs={{0,16},{2,18},{4,20},{6,22},{8,24},{10,26},{12,28},{14,30},{16,0},... | collective-permute-start | bytes 786440 | tf_op jit(solution)/shard_map/ppermute | solution.py:271
  66.2 21.6 %collective-permute-start.21 = (bf16[64,2048]{1,0:T(8,128)(2,1)}, bf16[64,2048]{1,0:T(8,128)(2,1)}, u32[]{:S(2)}, u32[]{:S(2)}) collective-permute-start(bf16[64,2048]{1,0:T(8,128)(2,1)} %bitcast.42), channel_id=1, source_target_pairs={{0,8},{2,10},{4,12},{6,14},{8,16},{10,18},{12,20},{14,22},{16,24},... | collective-permute-start | bytes 786440 | tf_op jit(solution)/shard_map/ppermute | solution.py:271
  68.8 21.4 %collective-permute-start.4 = (bf16[4,64,896]{2,1,0:T(8,128)(2,1)S(1)}, bf16[4,64,896]{2,1,0:T(8,128)(2,1)S(1)}, u32[]{:S(2)}, u32[]{:S(2)}) collective-permute-start(bf16[4,64,896]{2,1,0:T(8,128)(2,1)S(1)} %pad_maximum_fusion.12.refs_0_), channel_id=1, source_target_pairs={{0,2},{2,0},{4,6},{6,4},{8,10},{10,8},{12,14},{14,12},{16,18},{18,... | collective-permute-start | bytes 1376264 | tf_op jit(solution)/shard_map/ppermute | solution.py:266
  69.7 22.6 %collective-permute-start.5 = (bf16[4,64,896]{2,1,0:T(8,128)(2,1)S(1)}, bf16[4,64,896]{2,1,0:T(8,128)(2,1)S(1)}, u32[]{:S(2)}, u32[]{:S(2)}) collective-permute-start(bf16[4,64,896]{2,1,0:T(8,128)(2,1)S(1)} %collective-permute-done.3.refs_1_), channel_id=1, source_target_pairs={{0,2},{2,0},{4,6},{6,4},{8,10},{10,8},{12,14},{14,12},{16,18},{18,... | collective-permute-start | bytes 1376264 | tf_op jit(solution)/shard_map/ppermute | solution.py:266
  86.3 24.5 %collective-permute-start.6 = (bf16[512,1024]{1,0:T(8,128)(2,1)S(1)}, bf16[512,1024]{1,0:T(8,128)(2,1)S(1)}, u32[]{:S(2)}, u32[]{:S(2)}) collective-permute-start(bf16[512,1024]{1,0:T(8,128)(2,1)S(1)} %copy-done), channel_id=1, source_target_pairs={{0,1},{1,0},{2,3},{3,2},{4,5},{5,4},{6,7},{7,6},{8,9},{9,8},{10,11... | collective-permute-start | bytes 3145736 | tf_op jit(solution)/shard_map/ppermute | solution.py:266
  87.8 40.1 %collective-permute-start.11 = (bf16[4,64,1280]{2,1,0:T(8,128)(2,1)}, bf16[4,64,1280]{2,1,0:T(8,128)(2,1)}, u32[]{:S(2)}, u32[]{:S(2)}) collective-permute-start(bf16[4,64,1280]{2,1,0:T(8,128)(2,1)} %pad_maximum_fusion.10.refs_0_), channel_id=1, source_target_pairs={{0,2},{2,0},{4,6},{6,4},{8,10},{10,8},{12,14},{14,12},{16,18},{18,... | collective-permute-start | bytes 1966088 | tf_op jit(solution)/shard_map/ppermute | solution.py:266
  90.2 37.7 %collective-permute-start.18 = (bf16[4,64,2048]{2,1,0:T(8,128)(2,1)}, bf16[4,64,2048]{2,1,0:T(8,128)(2,1)}, u32[]{:S(2)}, u32[]{:S(2)}) collective-permute-start(bf16[4,64,2048]{2,1,0:T(8,128)(2,1)} %pad_maximum_fusion.7.refs_0_), channel_id=1, source_target_pairs={{0,4},{2,6},{4,0},{6,2},{8,12},{10,14},{12,8},{14,10},{16,20},{18,... | collective-permute-start | bytes 3145736 | tf_op jit(solution)/shard_map/ppermute | solution.py:266
  91.8 46.9 %collective-permute-start.24 = (bf16[4,64,2048]{2,1,0:T(8,128)(2,1)}, bf16[4,64,2048]{2,1,0:T(8,128)(2,1)}, u32[]{:S(2)}, u32[]{:S(2)}) collective-permute-start(bf16[4,64,2048]{2,1,0:T(8,128)(2,1)} %pad_maximum_fusion.8.refs_0_), channel_id=1, source_target_pairs={{0,4},{2,6},{4,0},{6,2},{8,12},{10,14},{12,8},{14,10},{16,20},{18,... | collective-permute-start | bytes 3145736 | tf_op jit(solution)/shard_map/ppermute | solution.py:266
  93.1 35.4 %collective-permute-start.12 = (bf16[4,64,1280]{2,1,0:T(8,128)(2,1)}, bf16[4,64,1280]{2,1,0:T(8,128)(2,1)}, u32[]{:S(2)}, u32[]{:S(2)}) collective-permute-start(bf16[4,64,1280]{2,1,0:T(8,128)(2,1)} %collective-permute-done.10.refs_1_), channel_id=1, source_target_pairs={{0,2},{2,0},{4,6},{6,4},{8,10},{10,8},{12,14},{14,12},{16,18},{18,... | collective-permute-start | bytes 1966088 | tf_op jit(solution)/shard_map/ppermute | solution.py:266
  111.4 27.2 %collective-permute-start.13 = (bf16[512,1024]{1,0:T(8,128)(2,1)S(1)}, bf16[512,1024]{1,0:T(8,128)(2,1)}, u32[]{:S(2)}, u32[]{:S(2)}) collective-permute-start(bf16[512,1024]{1,0:T(8,128)(2,1)S(1)} %copy-done.22), channel_id=1, source_target_pairs={{0,1},{1,0},{2,3},{3,2},{4,5},{5,4},{6,7},{7,6},{8,9},{9,8},{10,11... | collective-permute-start | bytes 3145736 | tf_op jit(solution)/shard_map/ppermute | solution.py:266
  128.0 27.9 %collective-permute-start.19 = (bf16[4,64,2048]{2,1,0:T(8,128)(2,1)}, bf16[4,64,2048]{2,1,0:T(8,128)(2,1)}, u32[]{:S(2)}, u32[]{:S(2)}) collective-permute-start(bf16[4,64,2048]{2,1,0:T(8,128)(2,1)} %pad_maximum_fusion.7.refs_0_), channel_id=1, source_target_pairs={{0,2},{2,0},{4,6},{6,4},{8,10},{10,8},{12,14},{14,12},{16,18},{18,... | collective-permute-start | bytes 3145736 | tf_op jit(solution)/shard_map/ppermute | solution.py:266
  128.0 32.8 %collective-permute-start.25 = (bf16[4,64,2048]{2,1,0:T(8,128)(2,1)}, bf16[4,64,2048]{2,1,0:T(8,128)(2,1)}, u32[]{:S(2)}, u32[]{:S(2)}) collective-permute-start(bf16[4,64,2048]{2,1,0:T(8,128)(2,1)} %pad_maximum_fusion.8.refs_0_), channel_id=1, source_target_pairs={{0,2},{2,0},{4,6},{6,4},{8,10},{10,8},{12,14},{14,12},{16,18},{18,... | collective-permute-start | bytes 3145736 | tf_op jit(solution)/shard_map/ppermute | solution.py:266
  128.5 27.4 %collective-permute-start.20 = (bf16[4,64,2048]{2,1,0:T(8,128)(2,1)}, bf16[4,64,2048]{2,1,0:T(8,128)(2,1)}, u32[]{:S(2)}, u32[]{:S(2)}) collective-permute-start(bf16[4,64,2048]{2,1,0:T(8,128)(2,1)} %collective-permute-done.18.refs_1_), channel_id=1, source_target_pairs={{0,2},{2,0},{4,6},{6,4},{8,10},{10,8},{12,14},{14,12},{16,18},{18,... | collective-permute-start | bytes 3145736 | tf_op jit(solution)/shard_map/ppermute | solution.py:266
  138.6 22.1 %collective-permute-start.26 = (bf16[4,64,2048]{2,1,0:T(8,128)(2,1)}, bf16[4,64,2048]{2,1,0:T(8,128)(2,1)}, u32[]{:S(2)}, u32[]{:S(2)}) collective-permute-start(bf16[4,64,2048]{2,1,0:T(8,128)(2,1)} %collective-permute-done.24.refs_1_), channel_id=1, source_target_pairs={{0,2},{2,0},{4,6},{6,4},{8,10},{10,8},{12,14},{14,12},{16,18},{18,... | collective-permute-start | bytes 3145736 | tf_op jit(solution)/shard_map/ppermute | solution.py:266
  151.5 25.9 %collective-permute-start.14 = (bf16[512,1024]{1,0:T(8,128)(2,1)}, bf16[512,1024]{1,0:T(8,128)(2,1)}, u32[]{:S(2)}, u32[]{:S(2)}) collective-permute-start(bf16[512,1024]{1,0:T(8,128)(2,1)} %convolution_convert_fusion.4), channel_id=1, source_target_pairs={{0,1},{1,0},{2,3},{3,2},{4,5},{5,4},{6,7},{7,6},{8,9},{9,8},{10,11... | collective-permute-start | bytes 3145736 | tf_op jit(solution)/shard_map/ppermute | solution.py:266
  180.4 24.7 %collective-permute-start.27 = (bf16[512,1024]{1,0:T(8,128)(2,1)S(1)}, bf16[512,1024]{1,0:T(8,128)(2,1)S(1)}, u32[]{:S(2)}, u32[]{:S(2)}) collective-permute-start(bf16[512,1024]{1,0:T(8,128)(2,1)S(1)} %get-tuple-element.179), channel_id=1, source_target_pairs={{0,1},{1,0},{2,3},{3,2},{4,5},{5,4},{6,7},{7,6},{8,9},{9,8},{10,11... | collective-permute-start | bytes 3145736 | tf_op jit(solution)/shard_map/ppermute | solution.py:266
  245.5 26.4 %collective-permute-start.29 = (bf16[512,1024]{1,0:T(8,128)(2,1)}, bf16[512,1024]{1,0:T(8,128)(2,1)}, u32[]{:S(2)}, u32[]{:S(2)}) collective-permute-start(bf16[512,1024]{1,0:T(8,128)(2,1)} %convolution_convert_fusion.5), channel_id=1, source_target_pairs={{0,1},{1,0},{2,3},{3,2},{4,5},{5,4},{6,7},{7,6},{8,9},{9,8},{10,11... | collective-permute-start | bytes 3145736 | tf_op jit(solution)/shard_map/ppermute | solution.py:266
  252.3 42.1 %collective-permute-start.28 = (bf16[512,1024]{1,0:T(8,128)(2,1)}, bf16[512,1024]{1,0:T(8,128)(2,1)}, u32[]{:S(2)}, u32[]{:S(2)}) collective-permute-start(bf16[512,1024]{1,0:T(8,128)(2,1)} %convolution_convert_fusion.6), channel_id=1, source_target_pairs={{0,1},{1,0},{2,3},{3,2},{4,5},{5,4},{6,7},{7,6},{8,9},{9,8},{10,11... | collective-permute-start | bytes 3145736 | tf_op jit(solution)/shard_map/ppermute | solution.py:266
  256.9 46.0 %collective-permute-start.48 = (bf16[4,2,64,2048]{3,2,0,1:T(8,128)(2,1)}, bf16[4,2,64,2048]{3,2,0,1:T(8,128)(2,1)}, u32[]{:S(2)}, u32[]{:S(2)}) collective-permute-start(bf16[4,2,64,2048]{3,2,0,1:T(8,128)(2,1)} %copy_bitcast_fusion), channel_id=1, source_target_pairs={{0,2},{2,0},{4,6},{6,4},{8,10},{10,8},{12,14},{14,12},{16,18},{18,... | collective-permute-start | bytes 6291464 | tf_op jit(solution)/shard_map/ppermute | solution.py:266
  260.2 47.1 %collective-permute-start.43 = (bf16[4,2,64,2048]{3,2,0,1:T(8,128)(2,1)}, bf16[4,2,64,2048]{3,2,0,1:T(8,128)(2,1)}, u32[]{:S(2)}, u32[]{:S(2)}) collective-permute-start(bf16[4,2,64,2048]{3,2,0,1:T(8,128)(2,1)} %copy_bitcast_fusion.1), channel_id=1, source_target_pairs={{0,2},{2,0},{4,6},{6,4},{8,10},{10,8},{12,14},{14,12},{16,18},{18,... | collective-permute-start | bytes 6291464 | tf_op jit(solution)/shard_map/ppermute | solution.py:266
  276.3 38.4 %collective-permute-start.30 = (bf16[512,1024]{1,0:T(8,128)(2,1)}, bf16[512,1024]{1,0:T(8,128)(2,1)}, u32[]{:S(2)}, u32[]{:S(2)}) collective-permute-start(bf16[512,1024]{1,0:T(8,128)(2,1)} %get-tuple-element.176), channel_id=1, source_target_pairs={{0,1},{1,0},{2,3},{3,2},{4,5},{5,4},{6,7},{7,6},{8,9},{9,8},{10,11... | collective-permute-start | bytes 3145736 | tf_op jit(solution)/shard_map/ppermute | solution.py:266
  305.9 71.4 %collective-permute-start.49 = (bf16[4,64,2048]{2,1,0:T(8,128)(2,1)}, bf16[4,64,2048]{2,1,0:T(8,128)(2,1)}, u32[]{:S(2)}, u32[]{:S(2)}) collective-permute-start(bf16[4,64,2048]{2,1,0:T(8,128)(2,1)} %fusion.46), channel_id=1, source_target_pairs={{0,4},{2,6},{4,0},{6,2},{8,12},{10,14},{12,8},{14,10},{16,20},{18,... | collective-permute-start | bytes 3145736 | tf_op jit(solution)/shard_map/ppermute | solution.py:266
  310.3 69.6 %collective-permute-start.44 = (bf16[4,64,2048]{2,1,0:T(8,128)(2,1)}, bf16[4,64,2048]{2,1,0:T(8,128)(2,1)}, u32[]{:S(2)}, u32[]{:S(2)}) collective-permute-start(bf16[4,64,2048]{2,1,0:T(8,128)(2,1)} %fusion.48), channel_id=1, source_target_pairs={{0,4},{2,6},{4,0},{6,2},{8,12},{10,14},{12,8},{14,10},{16,20},{18,... | collective-permute-start | bytes 3145736 | tf_op jit(solution)/shard_map/ppermute | solution.py:266
  363.2 11.5 %collective-permute-start.32 = (bf16[4,2,64,896]{3,2,0,1:T(8,128)(2,1)}, bf16[4,2,64,896]{3,2,0,1:T(8,128)(2,1)}, u32[]{:S(2)}, u32[]{:S(2)}) collective-permute-start(bf16[4,2,64,896]{3,2,0,1:T(8,128)(2,1)} %pad_maximum_fusion.9), channel_id=1, source_target_pairs={{0,2},{2,0},{4,6},{6,4},{8,10},{10,8},{12,14},{14,12},{16,18},{18,... | collective-permute-start | bytes 2752520 | tf_op jit(solution)/shard_map/ppermute | solution.py:266
  372.8 43.7 %collective-permute-start.38 = (bf16[4,2,64,1280]{3,2,0,1:T(8,128)(2,1)S(1)}, bf16[4,2,64,1280]{3,2,0,1:T(8,128)(2,1)S(1)}, u32[]{:S(2)}, u32[]{:S(2)}) collective-permute-start(bf16[4,2,64,1280]{3,2,0,1:T(8,128)(2,1)S(1)} %copy.177), channel_id=1, source_target_pairs={{0,2},{2,0},{4,6},{6,4},{8,10},{10,8},{12,14},{14,12},{16,18},{18,... | collective-permute-start | bytes 3932168 | tf_op jit(solution)/shard_map/ppermute | solution.py:266
  374.0 25.0 %collective-permute-start.31 = (bf16[512,1024]{1,0:T(8,128)(2,1)S(1)}, bf16[512,1024]{1,0:T(8,128)(2,1)S(1)}, u32[]{:S(2)}, u32[]{:S(2)}) collective-permute-start(bf16[512,1024]{1,0:T(8,128)(2,1)S(1)} %copy-done.42), channel_id=1, source_target_pairs={{0,1},{1,0},{2,3},{3,2},{4,5},{5,4},{6,7},{7,6},{8,9},{9,8},{10,11... | collective-permute-start | bytes 3145736 | tf_op jit(solution)/shard_map/ppermute | solution.py:266
  375.8 43.3 %collective-permute-start.33 = (bf16[4,64,896]{2,1,0:T(8,128)(2,1)S(1)}, bf16[4,64,896]{2,1,0:T(8,128)(2,1)S(1)}, u32[]{:S(2)}, u32[]{:S(2)}) collective-permute-start(bf16[4,64,896]{2,1,0:T(8,128)(2,1)S(1)} %fusion.89), channel_id=1, source_target_pairs={{0,4},{2,6},{4,0},{6,2},{8,12},{10,14},{12,8},{14,10},{16,20},{18,... | collective-permute-start | bytes 1376264 | tf_op jit(solution)/shard_map/ppermute | solution.py:266
  379.9 22.8 %collective-permute-start.50 = (bf16[64,2048]{1,0:T(8,128)(2,1)S(1)}, bf16[64,2048]{1,0:T(8,128)(2,1)S(1)}, u32[]{:S(2)}, u32[]{:S(2)}) collective-permute-start(bf16[64,2048]{1,0:T(8,128)(2,1)S(1)} %get-tuple-element.195), channel_id=1, source_target_pairs={{0,8},{2,10},{4,12},{6,14},{8,16},{10,18},{12,20},{14,22},{16,24},... | collective-permute-start | bytes 786440 | tf_op jit(solution)/shard_map/ppermute | solution.py:271
  380.0 22.8 %collective-permute-start.52 = (bf16[64,2048]{1,0:T(8,128)(2,1)S(1)}, bf16[64,2048]{1,0:T(8,128)(2,1)S(1)}, u32[]{:S(2)}, u32[]{:S(2)}) collective-permute-start(bf16[64,2048]{1,0:T(8,128)(2,1)S(1)} %get-tuple-element.196), channel_id=1, source_target_pairs={{0,24},{2,26},{4,28},{6,30},{8,0},{10,2},{12,4},{14,6},{16,8},{18,... | collective-permute-start | bytes 786440 | tf_op jit(solution)/shard_map/ppermute | solution.py:271
  399.0 16.5 %collective-permute-start.51 = (bf16[64,2048]{1,0:T(8,128)(2,1)S(1)}, bf16[64,2048]{1,0:T(8,128)(2,1)S(1)}, u32[]{:S(2)}, u32[]{:S(2)}) collective-permute-start(bf16[64,2048]{1,0:T(8,128)(2,1)S(1)} %get-tuple-element.197), channel_id=1, source_target_pairs={{0,16},{2,18},{4,20},{6,22},{8,24},{10,26},{12,28},{14,30},{16,0},... | collective-permute-start | bytes 786440 | tf_op jit(solution)/shard_map/ppermute | solution.py:271
  402.7 17.7 %collective-permute-start.45 = (bf16[64,2048]{1,0:T(8,128)(2,1)S(1)}, bf16[64,2048]{1,0:T(8,128)(2,1)S(1)}, u32[]{:S(2)}, u32[]{:S(2)}) collective-permute-start(bf16[64,2048]{1,0:T(8,128)(2,1)S(1)} %get-tuple-element.198), channel_id=1, source_target_pairs={{0,8},{2,10},{4,12},{6,14},{8,16},{10,18},{12,20},{14,22},{16,24},... | collective-permute-start | bytes 786440 | tf_op jit(solution)/shard_map/ppermute | solution.py:271
  402.7 21.5 %collective-permute-start.47 = (bf16[64,2048]{1,0:T(8,128)(2,1)S(1)}, bf16[64,2048]{1,0:T(8,128)(2,1)S(1)}, u32[]{:S(2)}, u32[]{:S(2)}) collective-permute-start(bf16[64,2048]{1,0:T(8,128)(2,1)S(1)} %get-tuple-element.199), channel_id=1, source_target_pairs={{0,24},{2,26},{4,28},{6,30},{8,0},{10,2},{12,4},{14,6},{16,8},{18,... | collective-permute-start | bytes 786440 | tf_op jit(solution)/shard_map/ppermute | solution.py:271
  415.5 21.8 %collective-permute-start.46 = (bf16[64,2048]{1,0:T(8,128)(2,1)S(1)}, bf16[64,2048]{1,0:T(8,128)(2,1)S(1)}, u32[]{:S(2)}, u32[]{:S(2)}) collective-permute-start(bf16[64,2048]{1,0:T(8,128)(2,1)S(1)} %get-tuple-element.200), channel_id=1, source_target_pairs={{0,16},{2,18},{4,20},{6,22},{8,24},{10,26},{12,28},{14,30},{16,0},... | collective-permute-start | bytes 786440 | tf_op jit(solution)/shard_map/ppermute | solution.py:271
  417.6 28.0 %collective-permute-start.39 = (bf16[4,64,1280]{2,1,0:T(8,128)(2,1)}, bf16[4,64,1280]{2,1,0:T(8,128)(2,1)}, u32[]{:S(2)}, u32[]{:S(2)}) collective-permute-start(bf16[4,64,1280]{2,1,0:T(8,128)(2,1)} %fusion.75), channel_id=1, source_target_pairs={{0,4},{2,6},{4,0},{6,2},{8,12},{10,14},{12,8},{14,10},{16,20},{18,... | collective-permute-start | bytes 1966088 | tf_op jit(solution)/shard_map/ppermute | solution.py:266
  420.4 17.8 %collective-permute-start.34 = (bf16[64,896]{1,0:T(8,128)(2,1)S(1)}, bf16[64,896]{1,0:T(8,128)(2,1)S(1)}, u32[]{:S(2)}, u32[]{:S(2)}) collective-permute-start(bf16[64,896]{1,0:T(8,128)(2,1)S(1)} %get-tuple-element.219), channel_id=1, source_target_pairs={{0,8},{2,10},{4,12},{6,14},{8,16},{10,18},{12,20},{14,22},{16,24},... | collective-permute-start | bytes 344072 | tf_op jit(solution)/shard_map/ppermute | solution.py:271
  420.4 17.8 %collective-permute-start.36 = (bf16[64,896]{1,0:T(8,128)(2,1)S(1)}, bf16[64,896]{1,0:T(8,128)(2,1)S(1)}, u32[]{:S(2)}, u32[]{:S(2)}) collective-permute-start(bf16[64,896]{1,0:T(8,128)(2,1)S(1)} %get-tuple-element.220), channel_id=1, source_target_pairs={{0,24},{2,26},{4,28},{6,30},{8,0},{10,2},{12,4},{14,6},{16,8},{18,... | collective-permute-start | bytes 344072 | tf_op jit(solution)/shard_map/ppermute | solution.py:271
  424.3 17.9 %collective-permute-start.35 = (bf16[64,896]{1,0:T(8,128)(2,1)S(1)}, bf16[64,896]{1,0:T(8,128)(2,1)S(1)}, u32[]{:S(2)}, u32[]{:S(2)}) collective-permute-start(bf16[64,896]{1,0:T(8,128)(2,1)S(1)} %get-tuple-element.221), channel_id=1, source_target_pairs={{0,16},{2,18},{4,20},{6,22},{8,24},{10,26},{12,28},{14,30},{16,0},... | collective-permute-start | bytes 344072 | tf_op jit(solution)/shard_map/ppermute | solution.py:271
  447.1 8.9 %collective-permute-start.40 = (bf16[64,1280]{1,0:T(8,128)(2,1)S(1)}, bf16[64,1280]{1,0:T(8,128)(2,1)S(1)}, u32[]{:S(2)}, u32[]{:S(2)}) collective-permute-start(bf16[64,1280]{1,0:T(8,128)(2,1)S(1)} %get-tuple-element.209), channel_id=1, source_target_pairs={{0,8},{2,10},{4,12},{6,14},{8,16},{10,18},{12,20},{14,22},{16,24},... | collective-permute-start | bytes 491528 | tf_op jit(solution)/shard_map/ppermute | solution.py:271
  447.1 11.6 %collective-permute-start.42 = (bf16[64,1280]{1,0:T(8,128)(2,1)S(1)}, bf16[64,1280]{1,0:T(8,128)(2,1)S(1)}, u32[]{:S(2)}, u32[]{:S(2)}) collective-permute-start(bf16[64,1280]{1,0:T(8,128)(2,1)S(1)} %get-tuple-element.210), channel_id=1, source_target_pairs={{0,24},{2,26},{4,28},{6,30},{8,0},{10,2},{12,4},{14,6},{16,8},{18,... | collective-permute-start | bytes 491528 | tf_op jit(solution)/shard_map/ppermute | solution.py:271
  450.9 11.8 %collective-permute-start.41 = (bf16[64,1280]{1,0:T(8,128)(2,1)S(1)}, bf16[64,1280]{1,0:T(8,128)(2,1)S(1)}, u32[]{:S(2)}, u32[]{:S(2)}) collective-permute-start(bf16[64,1280]{1,0:T(8,128)(2,1)S(1)} %get-tuple-element.211), channel_id=1, source_target_pairs={{0,16},{2,18},{4,20},{6,22},{8,24},{10,26},{12,28},{14,30},{16,0},... | collective-permute-start | bytes 491528 | tf_op jit(solution)/shard_map/ppermute | solution.py:271
  (70 other events, 693.2 us)

commit v2 on v1

--- a/solution.py
+++ b/solution.py
@@ -486,6 +486,7 @@
     scaled1_rest, _, pre_rest = normalize(
         tokens_rest.astype(jnp.float32), norm1_gain, norm1_offset
     )
+    scaled1, inverse1, scaled1_rest = tie(scaled1, inverse1, scaled1_rest)
     normed1 = jnp.concatenate(
         relative(jnp.concatenate([pre_own.astype(jnp.bfloat16), pre_rest.astype(jnp.bfloat16)]))
     )
@@ -590,9 +591,9 @@
     part_rest = first_grad([jnp.concatenate(blocks[1:]) for blocks in by_owner])
     (part_own,) = tie(first_grad([blocks[0] for blocks in by_owner]))
     grad_norm1 = scatter_tensor(part_own, part_rest)
-    seen_own, seen_rest, seen_scaled = tie(part_own, part_rest, scaled1)
+    seen_own, seen_rest = tie(part_own, part_rest)
     grad_ln1_gain, grad_ln1_bias = tie(
-        jnp.sum(seen_own * seen_scaled, axis=0) + jnp.sum(seen_rest * scaled1_rest, axis=0),
+        jnp.sum(seen_own * scaled1, axis=0) + jnp.sum(seen_rest * scaled1_rest, axis=0),
         jnp.sum(seen_own, axis=0) + jnp.sum(seen_rest, axis=0),
     )
     grad_qkv = []

time: 473 us -> 462 us (0.977)
  waiting for transfers between devices: 168 us -> 159 us
  other arithmetic: 51.6 us -> 59 us
  local copies, waits for them, and re-layouts: 43.7 us -> 37.8 us
    ppermute x24, waiting for transfers between devices: 86.5 us -> 78.5 us  [shift(): lax.ppermute(value, axis_name, [(i, (i + amount * step) % size) for i in...]
    ppermute x24, starting transfers between devices: 37.5 us -> 32.1 us  [shift(): lax.ppermute(value, axis_name, [(i, (i + amount * step) % size) for i in...]
    unnamed x135 -> x113, local copies, waits for them, and re-layouts: 17.5 us -> 12.7 us
  transfers between devices with their start and end apart: 53 -> 53, of which waited for: 22 -> 23; matrix products, arithmetic and copies ran while one was open for 27% -> 29% of each run, Pallas kernels for 11% -> 11%
where the time goes in v2:
time: 462 us; the launch traced here: 454 us
  waiting for transfers between devices  159 us (34%)
  matrix products  92 us (20%)
  other arithmetic  59 us (13%)
  starting transfers between devices  54 us (12%)
  Pallas kernels  50.5 us (11%)
  local copies, waits for them, and re-layouts  37.8 us (8%)
    ppermute x29, waiting for transfers between devices, flip(): lax.ppermute(value, axis_name, [(i, i ^ 1 << bit) for i in range(size)])  80.2 us
    ppermute x24, waiting for transfers between devices, shift(): lax.ppermute(value, axis_name, [(i, (i + amount * step) % size) for i in...  78.5 us
    dot_general x10, matrix products, contract_cols(): lax.dot_general(left_rows, right_rows, (((1,), (1,)), ((), ())), preferre...  33.9 us
    ppermute x24, starting transfers between devices, shift(): lax.ppermute(value, axis_name, [(i, (i + amount * step) % size) for i in...  32.1 us
    dot_general x5, matrix products, contract_rows(): lax.dot_general(left_rows, right_rows, (((0,), (0,)), ((), ())), preferre...  25.7 us
    ppermute x29, starting transfers between devices, flip(): lax.ppermute(value, axis_name, [(i, i ^ 1 << bit) for i in range(size)])  21.9 us
    pallas_call x2, Pallas kernels, attention_back(): pl.pallas_call(functools.partial(attention_back_kernel, tiles=tiles, bloc...  18.5 us
    pallas_call x4, Pallas kernels, place_blocks(): out = out(where, *pieces)  17.6 us
  transfers between devices with their start and end apart: 53, of which 23 were waited for; matrix products, arithmetic and copies ran while one was open for 29% of the time, Pallas kernels for 11%

profile of v2, /device:TPU:0, one launch (start us, length us, event | category | flops | bytes accessed | tf_op | source)
XLA Modules:
  0.0 454.1 jit_solution(4120227812110261996)
XLA Ops:
  5.2 5.1 %collective-permute-start.2 = (bf16[64,896]{1,0:T(8,128)(2,1)S(1)}, bf16[64,896]{1,0:T(8,128)(2,1)S(1)}, u32[]{:S(2)}, u32[]{:S(2)}) collective-permute-start(bf16[64,896]{1,0:T(8,128)(2,1)S(1)} %get-tuple-element.235), channel_id=1, source_target_pairs={{0,24},{2,26},{4,28},{6,30},{8,0},{10,2},{12,4},{14,6},{16,8},{18,... | collective-permute-start | bytes 344072 | tf_op jit(solution)/shard_map/ppermute | solution.py:271
  13.8 6.5 %collective-permute-done.1 = bf16[64,896]{1,0:T(8,128)(2,1)S(1)} collective-permute-done((bf16[64,896]{1,0:T(8,128)(2,1)S(1)}, bf16[64,896]{1,0:T(8,128)(2,1)S(1)}, u32[]{:S(2)}, u32[]{:S(2)}) %collective-permute-start.1) | collective-permute-done | bytes 114720 | tf_op jit(solution)/shard_map/ppermute | solution.py:271
  26.6 10.3 %collective-permute-done.8 = bf16[64,1280]{1,0:T(8,128)(2,1)S(1)} collective-permute-done((bf16[64,1280]{1,0:T(8,128)(2,1)S(1)}, bf16[64,1280]{1,0:T(8,128)(2,1)S(1)}, u32[]{:S(2)}, u32[]{:S(2)}) %collective-permute-start.8) | collective-permute-done | bytes 163872 | tf_op jit(solution)/shard_map/ppermute | solution.py:271
  44.0 17.3 %collective-permute-done.16 = bf16[64,2048]{1,0:T(8,128)(2,1)S(1)} collective-permute-done((bf16[64,2048]{1,0:T(8,128)(2,1)S(1)}, bf16[64,2048]{1,0:T(8,128)(2,1)S(1)}, u32[]{:S(2)}, u32[]{:S(2)}) %collective-permute-start.16) | collective-permute-done | bytes 262176 | tf_op jit(solution)/shard_map/ppermute | solution.py:271
  71.7 13.7 %collective-permute-done.22 = bf16[64,2048]{1,0:T(8,128)(2,1)} collective-permute-done((bf16[64,2048]{1,0:T(8,128)(2,1)S(1)}, bf16[64,2048]{1,0:T(8,128)(2,1)}, u32[]{:S(2)}, u32[]{:S(2)}) %collective-permute-start.22) | collective-permute-done | bytes 262176 | tf_op jit(solution)/shard_map/ppermute | solution.py:271
  91.1 3.6 place_blocks.4
  100.7 9.2 %collective-permute-done.6 = bf16[512,1024]{1,0:T(8,128)(2,1)S(1)} collective-permute-done((bf16[512,1024]{1,0:T(8,128)(2,1)S(1)}, bf16[512,1024]{1,0:T(8,128)(2,1)S(1)}, u32[]{:S(2)}, u32[]{:S(2)}) %collective-permute-start.6) | collective-permute-done | bytes 1048608 | tf_op jit(solution)/shard_map/ppermute | solution.py:266
  119.3 7.3 %attention.2 = (bf16[1024,256]{1,0:T(8,128)(2,1)}, f32[16,1024]{1,0:T(8,128)}) custom-call(s32[1,8]{1,0:T(1,128)} %lengths_ref.7, bf16[1024,768]{1,0:T(8,128)(2,1)} %add_convert_fusion.1.x_ref), custom_call_target="tpu_custom_call" | custom-call | tf_op jit(solution)/shard_map/attention/pallas_call | solution.py:195
  127.3 4.1 place_blocks.5
  131.4 4.7 %add_convert_fusion.x_ref = bf16[1024,768]{1,0:T(8,128)(2,1)} fusion(f32[768]{0:T(1024)S(1)} %add.542, bf16[1024,1280]{1,0:T(8,128)(2,1)} %bitcast.287, bf16[512,1024]{1,0:T(8,128)(2,1)} %copy-done.30, bf16[512,1024]{1,0:T(8,128)(2,1)S(1)} %get-tuple-element.191), kind=kOutput, calls=%fused_computation.30 | convolution fusion | flops 1616379904 | bytes 5245952 | tf_op jit(solution)/shard_map/dot_general | solution.py:496
  137.2 7.1 %attention.3 = (bf16[1024,256]{1,0:T(8,128)(2,1)}, f32[16,1024]{1,0:T(8,128)}) custom-call(s32[1,8]{1,0:T(1,128)} %lengths_ref.7, bf16[1024,768]{1,0:T(8,128)(2,1)} %add_convert_fusion.x_ref), custom_call_target="tpu_custom_call" | custom-call | tf_op jit(solution)/shard_map/attention/pallas_call | solution.py:195
  145.6 3.4 convolution_convert_fusion.4
  155.7 4.9 %place_blocks.6 = bf16[16,64,2048]{2,1,0:T(8,128)(2,1)} custom-call(s32[16]{0:T(128)} %pad_add_fusion.where_ref, bf16[4,64,2048]{2,1,0:T(8,128)(2,1)} %copy-done.15, bf16[4,64,2048]{2,1,0:T(8,128)(2,1)} %collective-permute-done.18.refs_1_, bf16[4,64,2048]{2,1,0:T(8,128)(2,1)} %collective-permute-done.19.refs_2_, ...), custom_call_target="tpu_custom_call" | custom-call | tf_op jit(solution)/shard_map/place_blocks/pallas_call | solution.py:302
  160.6 5.0 %place_blocks.7 = bf16[16,64,2048]{2,1,0:T(8,128)(2,1)} custom-call(s32[16]{0:T(128)} %pad_add_fusion.where_ref, bf16[4,64,2048]{2,1,0:T(8,128)(2,1)} %pad_maximum_fusion.8.refs_0_, bf16[4,64,2048]{2,1,0:T(8,128)(2,1)} %collective-permute-done.24.refs_1_, bf16[4,64,2048]{2,1,0:T(8,128)(2,1)} %collective-permute-done.25.refs_2_, ...), custom_call_target="tpu_custom_call" | custom-call | tf_op jit(solution)/shard_map/place_blocks/pallas_call | solution.py:302
  165.6 9.2 %collective-permute-done.14 = bf16[512,1024]{1,0:T(8,128)(2,1)} collective-permute-done((bf16[512,1024]{1,0:T(8,128)(2,1)}, bf16[512,1024]{1,0:T(8,128)(2,1)}, u32[]{:S(2)}, u32[]{:S(2)}) %collective-permute-start.14) | collective-permute-done | bytes 1048608 | tf_op jit(solution)/shard_map/ppermute | solution.py:266
  182.9 7.4 %fusion.112 = (f32[2048]{0:T(1024)S(1)}, bf16[512,2048]{1,0:T(8,128)(2,1)}) fusion(f32[512,2048]{1,0:T(8,128)S(1)} %fusion.118, f32[2048]{0:T(1024)S(1)} %add.554, bf16[512,1024]{1,0:T(8,128)(2,1)} %param.16, bf16[1024,2048]{1,0:T(8,128)(2,1)S(1)} %bitcast.294), kind=kOutput, calls=%fused_computation.251 | convolution fusion | flops 2169501696 | bytes 11550720 | tf_op jit(solution)/shard_map/dot_general | solution.py:532
  190.2 13.7 %collective-permute-done.27 = bf16[512,1024]{1,0:T(8,128)(2,1)S(1)} collective-permute-done((bf16[512,1024]{1,0:T(8,128)(2,1)S(1)}, bf16[512,1024]{1,0:T(8,128)(2,1)S(1)}, u32[]{:S(2)}, u32[]{:S(2)}) %collective-permute-start.27) | collective-permute-done | bytes 1048608 | tf_op jit(solution)/shard_map/ppermute | solution.py:266
  204.0 4.9 %multiply_convert_fusion = (bf16[512,2048]{1,0:T(8,128)(2,1)S(1)}, bf16[512,2048]{1,0:T(8,128)(2,1)S(1)}, f32[512,2048]{1,0:T(8,128)S(1)}) fusion(f32[2048]{0:T(1024)S(1)} %add.554, f32[512,2048]{1,0:T(8,128)S(1)} %fusion.118, bf16[512,1024]{1,0:T(8,128)(2,1)S(1)} %collective-permute-done.27, bf16[1024,2048]{1,0:T(8,128)(2,1)S(1)} %bitcast.299), kind=kOutput, calls=%fused_computation.26 | convolution fusion | flops 2168455168 | bytes 17833984 | tf_op jit(solution)/shard_map/dot_general | solution.py:531
  208.9 3.7 fusion.119
  212.6 6.9 %fusion.111 = (f32[2048]{0:T(1024)S(1)}, bf16[512,2048]{1,0:T(8,128)(2,1)}) fusion(f32[512,2048]{1,0:T(8,128)S(1)} %get-tuple-element.240, f32[2048]{0:T(1024)S(1)} %add.554, bf16[512,1024]{1,0:T(8,128)(2,1)} %collective-permute-done.13, bf16[1024,2048]{1,0:T(8,128)(2,1)S(1)} %bitcast.296), kind=kOutput, calls=%fused_computation.250 | convolution fusion | flops 2169501696 | bytes 11550720 | tf_op jit(solution)/shard_map/dot_general | solution.py:532
  219.5 7.9 %fusion.22 = bf16[1024,2048]{1,0:T(8,128)(2,1)} fusion(bf16[512,2048]{1,0:T(8,128)(2,1)S(1)} %get-tuple-element.67, bf16[512,2048]{1,0:T(8,128)(2,1)S(1)} %get-tuple-element.65, bf16[512,1024]{1,0:T(8,128)(2,1)} %collective-permute-done.13, bf16[512,1024]{1,0:T(8,128)(2,1)} %param.16), kind=kOutput, calls=%fused_computation.28 | convolution fusion | flops 4309647360 | bytes 10485760 | tf_op jit(solution)/shard_map/dot_general | solution.py:48
  227.4 6.3 %convolution_convert_fusion.5 = bf16[512,1024]{1,0:T(8,128)(2,1)} fusion(bf16[512,2048]{1,0:T(8,128)(2,1)} %get-tuple-element.71, bf16[1024,2048]{1,0:T(8,128)(2,1)} %bitcast.297), kind=kOutput, calls=%fused_computation.89 | convolution fusion | flops 2148007936 | bytes 7340032 | tf_op jit(solution)/shard_map/dot_general | solution.py:54
  233.7 3.8 fusion.120
  237.6 6.4 %fusion.25 = bf16[1024,2048]{1,0:T(8,128)(2,1)} fusion(bf16[512,2048]{1,0:T(8,128)(2,1)S(1)} %copy-done.52, bf16[512,2048]{1,0:T(8,128)(2,1)S(1)} %copy-done.50, bf16[512,1024]{1,0:T(8,128)(2,1)S(1)} %copy-done.49, bf16[512,1024]{1,0:T(8,128)(2,1)S(1)} %get-tuple-element.183), kind=kOutput, calls=%fused_computation.29 | convolution fusion | flops 4309647360 | bytes 10485760 | tf_op jit(solution)/shard_map/dot_general | solution.py:48
  245.3 6.1 %convolution_convert_fusion.6 = bf16[512,1024]{1,0:T(8,128)(2,1)} fusion(bf16[512,2048]{1,0:T(8,128)(2,1)} %copy-done.51, bf16[1024,2048]{1,0:T(8,128)(2,1)} %bitcast.293), kind=kOutput, calls=%fused_computation.90 | convolution fusion | flops 2148007936 | bytes 7340032 | tf_op jit(solution)/shard_map/dot_general | solution.py:54
  260.0 11.1 %collective-permute-done.29 = bf16[512,1024]{1,0:T(8,128)(2,1)} collective-permute-done((bf16[512,1024]{1,0:T(8,128)(2,1)}, bf16[512,1024]{1,0:T(8,128)(2,1)}, u32[]{:S(2)}, u32[]{:S(2)}) %collective-permute-start.29) | collective-permute-done | bytes 1048608 | tf_op jit(solution)/shard_map/ppermute | solution.py:266
  273.0 4.3 fusion.108
  277.8 15.7 %collective-permute-done.28 = bf16[512,1024]{1,0:T(8,128)(2,1)S(1)} collective-permute-done((bf16[512,1024]{1,0:T(8,128)(2,1)}, bf16[512,1024]{1,0:T(8,128)(2,1)S(1)}, u32[]{:S(2)}, u32[]{:S(2)}) %collective-permute-start.28) | collective-permute-done | bytes 1048608 | tf_op jit(solution)/shard_map/ppermute | solution.py:266
  297.0 3.4 add_add_fusion
  308.3 5.6 %collective-permute-done.30 = bf16[512,1024]{1,0:T(8,128)(2,1)} collective-permute-done((bf16[512,1024]{1,0:T(8,128)(2,1)}, bf16[512,1024]{1,0:T(8,128)(2,1)}, u32[]{:S(2)}, u32[]{:S(2)}) %collective-permute-start.30) | collective-permute-done | bytes 1048608 | tf_op jit(solution)/shard_map/ppermute | solution.py:266
  318.2 9.4 %attention_back.2 = (bf16[1024,768]{1,0:T(8,128)(2,1)}, f32[8,256]{1,0:T(8,128)}) custom-call(s32[1,8]{1,0:T(1,128)} %lengths_ref.7, bf16[1024,768]{1,0:T(8,128)(2,1)} %add_convert_fusion.1.x_ref, bf16[1024,256]{1,0:T(8,128)(2,1)} %get-tuple-element.58.o_ref, bf16[1024,256]{1,0:T(8,128)(2,1)} %get-tuple-element.209.do_ref, f32[16,1024]{1,0:T(8,128)} %get-tuple-element.73.lse_ref), custom_call_target="tpu_custom_call" | custom-call | tf_op jit(solution)/shard_map/attention_back/pallas_call | solution.py:226
  327.6 4.5 convolution_convert_fusion
  332.1 3.8 convolution_convert_fusion.2
  336.0 9.2 %attention_back.3 = (bf16[1024,768]{1,0:T(8,128)(2,1)}, f32[8,256]{1,0:T(8,128)}) custom-call(s32[1,8]{1,0:T(1,128)} %lengths_ref.7, bf16[1024,768]{1,0:T(8,128)(2,1)} %add_convert_fusion.x_ref, bf16[1024,256]{1,0:T(8,128)(2,1)} %get-tuple-element.62.o_ref, bf16[1024,256]{1,0:T(8,128)(2,1)} %get-tuple-element.210.do_ref, f32[16,1024]{1,0:T(8,128)} %get-tuple-element.75.lse_ref), custom_call_target="tpu_custom_call" | custom-call | tf_op jit(solution)/shard_map/attention_back/pallas_call | solution.py:226
  345.1 4.2 fusion.46
  364.4 3.9 fusion.102
  369.1 3.8 collective-permute-start.52
  373.0 3.9 fusion.104
  377.8 5.6 %collective-permute-done.31 = bf16[512,1024]{1,0:T(8,128)(2,1)S(1)} collective-permute-done((bf16[512,1024]{1,0:T(8,128)(2,1)S(1)}, bf16[512,1024]{1,0:T(8,128)(2,1)S(1)}, u32[]{:S(2)}, u32[]{:S(2)}) %collective-permute-start.31) | collective-permute-done | bytes 1048608 | tf_op jit(solution)/shard_map/ppermute | solution.py:266
  387.8 3.6 multiply_add_fusion.2
  394.4 3.9 collective-permute-start.47
  398.3 4.1 collective-permute-done.51
  404.6 3.4 collective-permute-done.39
  409.9 3.3 collective-permute-start.42
  413.6 11.5 %collective-permute-done.46 = bf16[64,2048]{1,0:T(8,128)(2,1)S(1)} collective-permute-done((bf16[64,2048]{1,0:T(8,128)(2,1)S(1)}, bf16[64,2048]{1,0:T(8,128)(2,1)S(1)}, u32[]{:S(2)}, u32[]{:S(2)}) %collective-permute-start.46) | collective-permute-done | bytes 262176 | tf_op jit(solution)/shard_map/ppermute | solution.py:271
  430.3 5.5 %collective-permute-done.33 = bf16[4,64,896]{2,1,0:T(8,128)(2,1)S(1)} collective-permute-done((bf16[4,64,896]{2,1,0:T(8,128)(2,1)S(1)}, bf16[4,64,896]{2,1,0:T(8,128)(2,1)S(1)}, u32[]{:S(2)}, u32[]{:S(2)}) %collective-permute-start.33) | collective-permute-done | bytes 458784 | tf_op jit(solution)/shard_map/ppermute | solution.py:266
  436.1 3.8 collective-permute-start.36
  442.7 3.7 collective-permute-done.35
  (339 shorter events, 142.2 us)
Async XLA Ops:
  5.2 8.7 %collective-permute-start.2 = (bf16[64,896]{1,0:T(8,128)(2,1)S(1)}, bf16[64,896]{1,0:T(8,128)(2,1)S(1)}, u32[]{:S(2)}, u32[]{:S(2)}) collective-permute-start(bf16[64,896]{1,0:T(8,128)(2,1)S(1)} %get-tuple-element.235), channel_id=1, source_target_pairs={{0,24},{2,26},{4,28},{6,30},{8,0},{10,2},{12,4},{14,6},{16,8},{18,... | collective-permute-start | bytes 344072 | tf_op jit(solution)/shard_map/ppermute | solution.py:271
  10.3 10.0 %collective-permute-start.1 = (bf16[64,896]{1,0:T(8,128)(2,1)S(1)}, bf16[64,896]{1,0:T(8,128)(2,1)S(1)}, u32[]{:S(2)}, u32[]{:S(2)}) collective-permute-start(bf16[64,896]{1,0:T(8,128)(2,1)S(1)} %get-tuple-element.235), channel_id=1, source_target_pairs={{0,16},{2,18},{4,20},{6,22},{8,24},{10,26},{12,28},{14,30},{16,0},... | collective-permute-start | bytes 344072 | tf_op jit(solution)/shard_map/ppermute | solution.py:271
  10.3 10.0 %collective-permute-start = (bf16[64,896]{1,0:T(8,128)(2,1)S(1)}, bf16[64,896]{1,0:T(8,128)(2,1)S(1)}, u32[]{:S(2)}, u32[]{:S(2)}) collective-permute-start(bf16[64,896]{1,0:T(8,128)(2,1)S(1)} %get-tuple-element.235), channel_id=1, source_target_pairs={{0,8},{2,10},{4,12},{6,14},{8,16},{10,18},{12,20},{14,22},{16,24},... | collective-permute-start | bytes 344072 | tf_op jit(solution)/shard_map/ppermute | solution.py:271
  22.0 14.9 %collective-permute-start.8 = (bf16[64,1280]{1,0:T(8,128)(2,1)S(1)}, bf16[64,1280]{1,0:T(8,128)(2,1)S(1)}, u32[]{:S(2)}, u32[]{:S(2)}) collective-permute-start(bf16[64,1280]{1,0:T(8,128)(2,1)S(1)} %pad_maximum_fusion.14), channel_id=1, source_target_pairs={{0,16},{2,18},{4,20},{6,22},{8,24},{10,26},{12,28},{14,30},{16,0},... | collective-permute-start | bytes 491528 | tf_op jit(solution)/shard_map/ppermute | solution.py:271
  22.7 14.2 %collective-permute-start.7 = (bf16[64,1280]{1,0:T(8,128)(2,1)S(1)}, bf16[64,1280]{1,0:T(8,128)(2,1)S(1)}, u32[]{:S(2)}, u32[]{:S(2)}) collective-permute-start(bf16[64,1280]{1,0:T(8,128)(2,1)S(1)} %pad_maximum_fusion.14), channel_id=1, source_target_pairs={{0,8},{2,10},{4,12},{6,14},{8,16},{10,18},{12,20},{14,22},{16,24},... | collective-permute-start | bytes 491528 | tf_op jit(solution)/shard_map/ppermute | solution.py:271
  36.9 7.0 %collective-permute-start.17 = (bf16[64,2048]{1,0:T(8,128)(2,1)S(1)}, bf16[64,2048]{1,0:T(8,128)(2,1)S(1)}, u32[]{:S(2)}, u32[]{:S(2)}) collective-permute-start(bf16[64,2048]{1,0:T(8,128)(2,1)S(1)} %copy-done.39), channel_id=1, source_target_pairs={{0,24},{2,26},{4,28},{6,30},{8,0},{10,2},{12,4},{14,6},{16,8},{18,... | collective-permute-start | bytes 786440 | tf_op jit(solution)/shard_map/ppermute | solution.py:271
  36.9 24.3 %collective-permute-start.16 = (bf16[64,2048]{1,0:T(8,128)(2,1)S(1)}, bf16[64,2048]{1,0:T(8,128)(2,1)S(1)}, u32[]{:S(2)}, u32[]{:S(2)}) collective-permute-start(bf16[64,2048]{1,0:T(8,128)(2,1)S(1)} %copy-done.39), channel_id=1, source_target_pairs={{0,16},{2,18},{4,20},{6,22},{8,24},{10,26},{12,28},{14,30},{16,0},... | collective-permute-start | bytes 786440 | tf_op jit(solution)/shard_map/ppermute | solution.py:271
  37.9 23.3 %collective-permute-start.15 = (bf16[64,2048]{1,0:T(8,128)(2,1)S(1)}, bf16[64,2048]{1,0:T(8,128)(2,1)S(1)}, u32[]{:S(2)}, u32[]{:S(2)}) collective-permute-start(bf16[64,2048]{1,0:T(8,128)(2,1)S(1)} %copy-done.39), channel_id=1, source_target_pairs={{0,8},{2,10},{4,12},{6,14},{8,16},{10,18},{12,20},{14,22},{16,24},... | collective-permute-start | bytes 786440 | tf_op jit(solution)/shard_map/ppermute | solution.py:271
  40.8 26.3 %collective-permute-start.3 = (bf16[4,64,896]{2,1,0:T(8,128)(2,1)}, bf16[4,64,896]{2,1,0:T(8,128)(2,1)}, u32[]{:S(2)}, u32[]{:S(2)}) collective-permute-start(bf16[4,64,896]{2,1,0:T(8,128)(2,1)} %pad_maximum_fusion.12.refs_0_), channel_id=1, source_target_pairs={{0,4},{2,6},{4,0},{6,2},{8,12},{10,14},{12,8},{14,10},{16,20},{18,... | collective-permute-start | bytes 1376264 | tf_op jit(solution)/shard_map/ppermute | solution.py:266
  61.3 8.5 %collective-permute-start.23 = (bf16[64,2048]{1,0:T(8,128)(2,1)S(1)}, bf16[64,2048]{1,0:T(8,128)(2,1)S(1)}, u32[]{:S(2)}, u32[]{:S(2)}) collective-permute-start(bf16[64,2048]{1,0:T(8,128)(2,1)S(1)} %bitcast.327), channel_id=1, source_target_pairs={{0,24},{2,26},{4,28},{6,30},{8,0},{10,2},{12,4},{14,6},{16,8},{18,... | collective-permute-start | bytes 786440 | tf_op jit(solution)/shard_map/ppermute | solution.py:271
  62.3 28.3 %collective-permute-start.10 = (bf16[4,64,1280]{2,1,0:T(8,128)(2,1)}, bf16[4,64,1280]{2,1,0:T(8,128)(2,1)}, u32[]{:S(2)}, u32[]{:S(2)}) collective-permute-start(bf16[4,64,1280]{2,1,0:T(8,128)(2,1)} %pad_maximum_fusion.10.refs_0_), channel_id=1, source_target_pairs={{0,4},{2,6},{4,0},{6,2},{8,12},{10,14},{12,8},{14,10},{16,20},{18,... | collective-permute-start | bytes 1966088 | tf_op jit(solution)/shard_map/ppermute | solution.py:266
  63.8 21.6 %collective-permute-start.22 = (bf16[64,2048]{1,0:T(8,128)(2,1)S(1)}, bf16[64,2048]{1,0:T(8,128)(2,1)}, u32[]{:S(2)}, u32[]{:S(2)}) collective-permute-start(bf16[64,2048]{1,0:T(8,128)(2,1)S(1)} %bitcast.328), channel_id=1, source_target_pairs={{0,16},{2,18},{4,20},{6,22},{8,24},{10,26},{12,28},{14,30},{16,0},... | collective-permute-start | bytes 786440 | tf_op jit(solution)/shard_map/ppermute | solution.py:271
  64.4 22.5 %collective-permute-start.21 = (bf16[64,2048]{1,0:T(8,128)(2,1)S(1)}, bf16[64,2048]{1,0:T(8,128)(2,1)}, u32[]{:S(2)}, u32[]{:S(2)}) collective-permute-start(bf16[64,2048]{1,0:T(8,128)(2,1)S(1)} %bitcast.329), channel_id=1, source_target_pairs={{0,8},{2,10},{4,12},{6,14},{8,16},{10,18},{12,20},{14,22},{16,24},... | collective-permute-start | bytes 786440 | tf_op jit(solution)/shard_map/ppermute | solution.py:271
  67.1 22.0 %collective-permute-start.4 = (bf16[4,64,896]{2,1,0:T(8,128)(2,1)}, bf16[4,64,896]{2,1,0:T(8,128)(2,1)}, u32[]{:S(2)}, u32[]{:S(2)}) collective-permute-start(bf16[4,64,896]{2,1,0:T(8,128)(2,1)} %pad_maximum_fusion.12.refs_0_), channel_id=1, source_target_pairs={{0,2},{2,0},{4,6},{6,4},{8,10},{10,8},{12,14},{14,12},{16,18},{18,... | collective-permute-start | bytes 1376264 | tf_op jit(solution)/shard_map/ppermute | solution.py:266
  69.8 21.4 %collective-permute-start.5 = (bf16[4,64,896]{2,1,0:T(8,128)(2,1)}, bf16[4,64,896]{2,1,0:T(8,128)(2,1)}, u32[]{:S(2)}, u32[]{:S(2)}) collective-permute-start(bf16[4,64,896]{2,1,0:T(8,128)(2,1)} %collective-permute-done.3.refs_1_), channel_id=1, source_target_pairs={{0,2},{2,0},{4,6},{6,4},{8,10},{10,8},{12,14},{14,12},{16,18},{18,... | collective-permute-start | bytes 1376264 | tf_op jit(solution)/shard_map/ppermute | solution.py:266
  85.4 24.5 %collective-permute-start.6 = (bf16[512,1024]{1,0:T(8,128)(2,1)S(1)}, bf16[512,1024]{1,0:T(8,128)(2,1)S(1)}, u32[]{:S(2)}, u32[]{:S(2)}) collective-permute-start(bf16[512,1024]{1,0:T(8,128)(2,1)S(1)} %copy-done.7), channel_id=1, source_target_pairs={{0,1},{1,0},{2,3},{3,2},{4,5},{5,4},{6,7},{7,6},{8,9},{9,8},{10,11... | collective-permute-start | bytes 3145736 | tf_op jit(solution)/shard_map/ppermute | solution.py:266
  86.9 39.7 %collective-permute-start.11 = (bf16[4,64,1280]{2,1,0:T(8,128)(2,1)}, bf16[4,64,1280]{2,1,0:T(8,128)(2,1)}, u32[]{:S(2)}, u32[]{:S(2)}) collective-permute-start(bf16[4,64,1280]{2,1,0:T(8,128)(2,1)} %pad_maximum_fusion.10.refs_0_), channel_id=1, source_target_pairs={{0,2},{2,0},{4,6},{6,4},{8,10},{10,8},{12,14},{14,12},{16,18},{18,... | collective-permute-start | bytes 1966088 | tf_op jit(solution)/shard_map/ppermute | solution.py:266
  89.1 37.6 %collective-permute-start.18 = (bf16[4,64,2048]{2,1,0:T(8,128)(2,1)S(1)}, bf16[4,64,2048]{2,1,0:T(8,128)(2,1)}, u32[]{:S(2)}, u32[]{:S(2)}) collective-permute-start(bf16[4,64,2048]{2,1,0:T(8,128)(2,1)S(1)} %pad_maximum_fusion.7.refs_0_), channel_id=1, source_target_pairs={{0,4},{2,6},{4,0},{6,2},{8,12},{10,14},{12,8},{14,10},{16,20},{18,... | collective-permute-start | bytes 3145736 | tf_op jit(solution)/shard_map/ppermute | solution.py:266
  90.6 46.6 %collective-permute-start.24 = (bf16[4,64,2048]{2,1,0:T(8,128)(2,1)}, bf16[4,64,2048]{2,1,0:T(8,128)(2,1)}, u32[]{:S(2)}, u32[]{:S(2)}) collective-permute-start(bf16[4,64,2048]{2,1,0:T(8,128)(2,1)} %pad_maximum_fusion.8.refs_0_), channel_id=1, source_target_pairs={{0,4},{2,6},{4,0},{6,2},{8,12},{10,14},{12,8},{14,10},{16,20},{18,... | collective-permute-start | bytes 3145736 | tf_op jit(solution)/shard_map/ppermute | solution.py:266
  91.1 36.1 %collective-permute-start.12 = (bf16[4,64,1280]{2,1,0:T(8,128)(2,1)}, bf16[4,64,1280]{2,1,0:T(8,128)(2,1)}, u32[]{:S(2)}, u32[]{:S(2)}) collective-permute-start(bf16[4,64,1280]{2,1,0:T(8,128)(2,1)} %collective-permute-done.10.refs_1_), channel_id=1, source_target_pairs={{0,2},{2,0},{4,6},{6,4},{8,10},{10,8},{12,14},{14,12},{16,18},{18,... | collective-permute-start | bytes 1966088 | tf_op jit(solution)/shard_map/ppermute | solution.py:266
  110.5 26.7 %collective-permute-start.13 = (bf16[512,1024]{1,0:T(8,128)(2,1)}, bf16[512,1024]{1,0:T(8,128)(2,1)}, u32[]{:S(2)}, u32[]{:S(2)}) collective-permute-start(bf16[512,1024]{1,0:T(8,128)(2,1)} %param.16), channel_id=1, source_target_pairs={{0,1},{1,0},{2,3},{3,2},{4,5},{5,4},{6,7},{7,6},{8,9},{9,8},{10,11... | collective-permute-start | bytes 3145736 | tf_op jit(solution)/shard_map/ppermute | solution.py:266
  126.6 29.1 %collective-permute-start.19 = (bf16[4,64,2048]{2,1,0:T(8,128)(2,1)S(1)}, bf16[4,64,2048]{2,1,0:T(8,128)(2,1)}, u32[]{:S(2)}, u32[]{:S(2)}) collective-permute-start(bf16[4,64,2048]{2,1,0:T(8,128)(2,1)S(1)} %pad_maximum_fusion.7.refs_0_), channel_id=1, source_target_pairs={{0,2},{2,0},{4,6},{6,4},{8,10},{10,8},{12,14},{14,12},{16,18},{18,... | collective-permute-start | bytes 3145736 | tf_op jit(solution)/shard_map/ppermute | solution.py:266
  126.7 33.9 %collective-permute-start.25 = (bf16[4,64,2048]{2,1,0:T(8,128)(2,1)}, bf16[4,64,2048]{2,1,0:T(8,128)(2,1)}, u32[]{:S(2)}, u32[]{:S(2)}) collective-permute-start(bf16[4,64,2048]{2,1,0:T(8,128)(2,1)} %pad_maximum_fusion.8.refs_0_), channel_id=1, source_target_pairs={{0,2},{2,0},{4,6},{6,4},{8,10},{10,8},{12,14},{14,12},{16,18},{18,... | collective-permute-start | bytes 3145736 | tf_op jit(solution)/shard_map/ppermute | solution.py:266
  127.2 28.5 %collective-permute-start.20 = (bf16[4,64,2048]{2,1,0:T(8,128)(2,1)}, bf16[4,64,2048]{2,1,0:T(8,128)(2,1)}, u32[]{:S(2)}, u32[]{:S(2)}) collective-permute-start(bf16[4,64,2048]{2,1,0:T(8,128)(2,1)} %collective-permute-done.18.refs_1_), channel_id=1, source_target_pairs={{0,2},{2,0},{4,6},{6,4},{8,10},{10,8},{12,14},{14,12},{16,18},{18,... | collective-permute-start | bytes 3145736 | tf_op jit(solution)/shard_map/ppermute | solution.py:266
  137.2 23.4 %collective-permute-start.26 = (bf16[4,64,2048]{2,1,0:T(8,128)(2,1)}, bf16[4,64,2048]{2,1,0:T(8,128)(2,1)}, u32[]{:S(2)}, u32[]{:S(2)}) collective-permute-start(bf16[4,64,2048]{2,1,0:T(8,128)(2,1)} %collective-permute-done.24.refs_1_), channel_id=1, source_target_pairs={{0,2},{2,0},{4,6},{6,4},{8,10},{10,8},{12,14},{14,12},{16,18},{18,... | collective-permute-start | bytes 3145736 | tf_op jit(solution)/shard_map/ppermute | solution.py:266
  149.0 25.9 %collective-permute-start.14 = (bf16[512,1024]{1,0:T(8,128)(2,1)}, bf16[512,1024]{1,0:T(8,128)(2,1)}, u32[]{:S(2)}, u32[]{:S(2)}) collective-permute-start(bf16[512,1024]{1,0:T(8,128)(2,1)} %convolution_convert_fusion.4), channel_id=1, source_target_pairs={{0,1},{1,0},{2,3},{3,2},{4,5},{5,4},{6,7},{7,6},{8,9},{9,8},{10,11... | collective-permute-start | bytes 3145736 | tf_op jit(solution)/shard_map/ppermute | solution.py:266
  179.3 24.7 %collective-permute-start.27 = (bf16[512,1024]{1,0:T(8,128)(2,1)S(1)}, bf16[512,1024]{1,0:T(8,128)(2,1)S(1)}, u32[]{:S(2)}, u32[]{:S(2)}) collective-permute-start(bf16[512,1024]{1,0:T(8,128)(2,1)S(1)} %get-tuple-element.183), channel_id=1, source_target_pairs={{0,1},{1,0},{2,3},{3,2},{4,5},{5,4},{6,7},{7,6},{8,9},{9,8},{10,11... | collective-permute-start | bytes 3145736 | tf_op jit(solution)/shard_map/ppermute | solution.py:266
  244.7 26.4 %collective-permute-start.29 = (bf16[512,1024]{1,0:T(8,128)(2,1)}, bf16[512,1024]{1,0:T(8,128)(2,1)}, u32[]{:S(2)}, u32[]{:S(2)}) collective-permute-start(bf16[512,1024]{1,0:T(8,128)(2,1)} %convolution_convert_fusion.5), channel_id=1, source_target_pairs={{0,1},{1,0},{2,3},{3,2},{4,5},{5,4},{6,7},{7,6},{8,9},{9,8},{10,11... | collective-permute-start | bytes 3145736 | tf_op jit(solution)/shard_map/ppermute | solution.py:266
  251.4 42.1 %collective-permute-start.28 = (bf16[512,1024]{1,0:T(8,128)(2,1)}, bf16[512,1024]{1,0:T(8,128)(2,1)S(1)}, u32[]{:S(2)}, u32[]{:S(2)}) collective-permute-start(bf16[512,1024]{1,0:T(8,128)(2,1)} %convolution_convert_fusion.6), channel_id=1, source_target_pairs={{0,1},{1,0},{2,3},{3,2},{4,5},{5,4},{6,7},{7,6},{8,9},{9,8},{10,11... | collective-permute-start | bytes 3145736 | tf_op jit(solution)/shard_map/ppermute | solution.py:266
  256.2 44.2 %collective-permute-start.48 = (bf16[4,2,64,2048]{3,2,0,1:T(8,128)(2,1)}, bf16[4,2,64,2048]{3,2,0,1:T(8,128)(2,1)}, u32[]{:S(2)}, u32[]{:S(2)}) collective-permute-start(bf16[4,2,64,2048]{3,2,0,1:T(8,128)(2,1)} %copy_bitcast_fusion), channel_id=1, source_target_pairs={{0,2},{2,0},{4,6},{6,4},{8,10},{10,8},{12,14},{14,12},{16,18},{18,... | collective-permute-start | bytes 6291464 | tf_op jit(solution)/shard_map/ppermute | solution.py:266
  259.5 45.3 %collective-permute-start.43 = (bf16[4,2,64,2048]{3,2,0,1:T(8,128)(2,1)}, bf16[4,2,64,2048]{3,2,0,1:T(8,128)(2,1)}, u32[]{:S(2)}, u32[]{:S(2)}) collective-permute-start(bf16[4,2,64,2048]{3,2,0,1:T(8,128)(2,1)} %copy_bitcast_fusion.1), channel_id=1, source_target_pairs={{0,2},{2,0},{4,6},{6,4},{8,10},{10,8},{12,14},{14,12},{16,18},{18,... | collective-permute-start | bytes 6291464 | tf_op jit(solution)/shard_map/ppermute | solution.py:266
  277.3 36.6 %collective-permute-start.30 = (bf16[512,1024]{1,0:T(8,128)(2,1)}, bf16[512,1024]{1,0:T(8,128)(2,1)}, u32[]{:S(2)}, u32[]{:S(2)}) collective-permute-start(bf16[512,1024]{1,0:T(8,128)(2,1)} %get-tuple-element.180), channel_id=1, source_target_pairs={{0,1},{1,0},{2,3},{3,2},{4,5},{5,4},{6,7},{7,6},{8,9},{9,8},{10,11... | collective-permute-start | bytes 3145736 | tf_op jit(solution)/shard_map/ppermute | solution.py:266
  303.3 61.0 %collective-permute-start.49 = (bf16[4,64,2048]{2,1,0:T(8,128)(2,1)}, bf16[4,64,2048]{2,1,0:T(8,128)(2,1)}, u32[]{:S(2)}, u32[]{:S(2)}) collective-permute-start(bf16[4,64,2048]{2,1,0:T(8,128)(2,1)} %fusion.41), channel_id=1, source_target_pairs={{0,4},{2,6},{4,0},{6,2},{8,12},{10,14},{12,8},{14,10},{16,20},{18,... | collective-permute-start | bytes 3145736 | tf_op jit(solution)/shard_map/ppermute | solution.py:266
  307.7 65.2 %collective-permute-start.44 = (bf16[4,64,2048]{2,1,0:T(8,128)(2,1)}, bf16[4,64,2048]{2,1,0:T(8,128)(2,1)}, u32[]{:S(2)}, u32[]{:S(2)}) collective-permute-start(bf16[4,64,2048]{2,1,0:T(8,128)(2,1)} %fusion.43), channel_id=1, source_target_pairs={{0,4},{2,6},{4,0},{6,2},{8,12},{10,14},{12,8},{14,10},{16,20},{18,... | collective-permute-start | bytes 3145736 | tf_op jit(solution)/shard_map/ppermute | solution.py:266
  355.1 36.3 %collective-permute-start.38 = (bf16[4,2,64,1280]{3,2,0,1:T(8,128)(2,1)}, bf16[4,2,64,1280]{3,2,0,1:T(8,128)(2,1)}, u32[]{:S(2)}, u32[]{:S(2)}) collective-permute-start(bf16[4,2,64,1280]{3,2,0,1:T(8,128)(2,1)} %copy.177), channel_id=1, source_target_pairs={{0,2},{2,0},{4,6},{6,4},{8,10},{10,8},{12,14},{14,12},{16,18},{18,... | collective-permute-start | bytes 3932168 | tf_op jit(solution)/shard_map/ppermute | solution.py:266
  358.9 24.5 %collective-permute-start.31 = (bf16[512,1024]{1,0:T(8,128)(2,1)S(1)}, bf16[512,1024]{1,0:T(8,128)(2,1)S(1)}, u32[]{:S(2)}, u32[]{:S(2)}) collective-permute-start(bf16[512,1024]{1,0:T(8,128)(2,1)S(1)} %get-tuple-element.243), channel_id=1, source_target_pairs={{0,1},{1,0},{2,3},{3,2},{4,5},{5,4},{6,7},{7,6},{8,9},{9,8},{10,11... | collective-permute-start | bytes 3145736 | tf_op jit(solution)/shard_map/ppermute | solution.py:266
  369.1 25.3 %collective-permute-start.50 = (bf16[64,2048]{1,0:T(8,128)(2,1)}, bf16[64,2048]{1,0:T(8,128)(2,1)}, u32[]{:S(2)}, u32[]{:S(2)}) collective-permute-start(bf16[64,2048]{1,0:T(8,128)(2,1)} %get-tuple-element.201), channel_id=1, source_target_pairs={{0,8},{2,10},{4,12},{6,14},{8,16},{10,18},{12,20},{14,22},{16,24},... | collective-permute-start | bytes 786440 | tf_op jit(solution)/shard_map/ppermute | solution.py:271
  369.1 29.1 %collective-permute-start.52 = (bf16[64,2048]{1,0:T(8,128)(2,1)}, bf16[64,2048]{1,0:T(8,128)(2,1)}, u32[]{:S(2)}, u32[]{:S(2)}) collective-permute-start(bf16[64,2048]{1,0:T(8,128)(2,1)} %get-tuple-element.202), channel_id=1, source_target_pairs={{0,24},{2,26},{4,28},{6,30},{8,0},{10,2},{12,4},{14,6},{16,8},{18,... | collective-permute-start | bytes 786440 | tf_op jit(solution)/shard_map/ppermute | solution.py:271
  373.0 29.4 %collective-permute-start.51 = (bf16[64,2048]{1,0:T(8,128)(2,1)}, bf16[64,2048]{1,0:T(8,128)(2,1)}, u32[]{:S(2)}, u32[]{:S(2)}) collective-permute-start(bf16[64,2048]{1,0:T(8,128)(2,1)} %get-tuple-element.203), channel_id=1, source_target_pairs={{0,16},{2,18},{4,20},{6,22},{8,24},{10,26},{12,28},{14,30},{16,0},... | collective-permute-start | bytes 786440 | tf_op jit(solution)/shard_map/ppermute | solution.py:271
  383.4 26.5 %collective-permute-start.45 = (bf16[64,2048]{1,0:T(8,128)(2,1)}, bf16[64,2048]{1,0:T(8,128)(2,1)}, u32[]{:S(2)}, u32[]{:S(2)}) collective-permute-start(bf16[64,2048]{1,0:T(8,128)(2,1)} %get-tuple-element.204), channel_id=1, source_target_pairs={{0,8},{2,10},{4,12},{6,14},{8,16},{10,18},{12,20},{14,22},{16,24},... | collective-permute-start | bytes 786440 | tf_op jit(solution)/shard_map/ppermute | solution.py:271
  392.7 15.3 %collective-permute-start.39 = (bf16[4,64,1280]{2,1,0:T(8,128)(2,1)S(1)}, bf16[4,64,1280]{2,1,0:T(8,128)(2,1)S(1)}, u32[]{:S(2)}, u32[]{:S(2)}) collective-permute-start(bf16[4,64,1280]{2,1,0:T(8,128)(2,1)S(1)} %fusion.70), channel_id=1, source_target_pairs={{0,4},{2,6},{4,0},{6,2},{8,12},{10,14},{12,8},{14,10},{16,20},{18,... | collective-permute-start | bytes 1966088 | tf_op jit(solution)/shard_map/ppermute | solution.py:266
  394.4 18.9 %collective-permute-start.47 = (bf16[64,2048]{1,0:T(8,128)(2,1)S(1)}, bf16[64,2048]{1,0:T(8,128)(2,1)S(1)}, u32[]{:S(2)}, u32[]{:S(2)}) collective-permute-start(bf16[64,2048]{1,0:T(8,128)(2,1)S(1)} %copy-done.38), channel_id=1, source_target_pairs={{0,24},{2,26},{4,28},{6,30},{8,0},{10,2},{12,4},{14,6},{16,8},{18,... | collective-permute-start | bytes 786440 | tf_op jit(solution)/shard_map/ppermute | solution.py:271
  398.3 26.8 %collective-permute-start.46 = (bf16[64,2048]{1,0:T(8,128)(2,1)S(1)}, bf16[64,2048]{1,0:T(8,128)(2,1)S(1)}, u32[]{:S(2)}, u32[]{:S(2)}) collective-permute-start(bf16[64,2048]{1,0:T(8,128)(2,1)S(1)} %copy-done.37), channel_id=1, source_target_pairs={{0,16},{2,18},{4,20},{6,22},{8,24},{10,26},{12,28},{14,30},{16,0},... | collective-permute-start | bytes 786440 | tf_op jit(solution)/shard_map/ppermute | solution.py:271
  402.4 24.7 %collective-permute-start.32 = (bf16[4,2,64,896]{3,2,0,1:T(8,128)(2,1)S(1)}, bf16[4,2,64,896]{3,2,0,1:T(8,128)(2,1)S(1)}, u32[]{:S(2)}, u32[]{:S(2)}) collective-permute-start(bf16[4,2,64,896]{3,2,0,1:T(8,128)(2,1)S(1)} %pad_maximum_fusion.9), channel_id=1, source_target_pairs={{0,2},{2,0},{4,6},{6,4},{8,10},{10,8},{12,14},{14,12},{16,18},{18,... | collective-permute-start | bytes 2752520 | tf_op jit(solution)/shard_map/ppermute | solution.py:266
  409.4 19.4 %collective-permute-start.40 = (bf16[64,1280]{1,0:T(8,128)(2,1)S(1)}, bf16[64,1280]{1,0:T(8,128)(2,1)S(1)}, u32[]{:S(2)}, u32[]{:S(2)}) collective-permute-start(bf16[64,1280]{1,0:T(8,128)(2,1)S(1)} %get-tuple-element.215), channel_id=1, source_target_pairs={{0,8},{2,10},{4,12},{6,14},{8,16},{10,18},{12,20},{14,22},{16,24},... | collective-permute-start | bytes 491528 | tf_op jit(solution)/shard_map/ppermute | solution.py:271
  409.9 18.9 %collective-permute-start.42 = (bf16[64,1280]{1,0:T(8,128)(2,1)S(1)}, bf16[64,1280]{1,0:T(8,128)(2,1)S(1)}, u32[]{:S(2)}, u32[]{:S(2)}) collective-permute-start(bf16[64,1280]{1,0:T(8,128)(2,1)S(1)} %get-tuple-element.216), channel_id=1, source_target_pairs={{0,24},{2,26},{4,28},{6,30},{8,0},{10,2},{12,4},{14,6},{16,8},{18,... | collective-permute-start | bytes 491528 | tf_op jit(solution)/shard_map/ppermute | solution.py:271
  413.3 16.9 %collective-permute-start.41 = (bf16[64,1280]{1,0:T(8,128)(2,1)S(1)}, bf16[64,1280]{1,0:T(8,128)(2,1)S(1)}, u32[]{:S(2)}, u32[]{:S(2)}) collective-permute-start(bf16[64,1280]{1,0:T(8,128)(2,1)S(1)} %get-tuple-element.217), channel_id=1, source_target_pairs={{0,16},{2,18},{4,20},{6,22},{8,24},{10,26},{12,28},{14,30},{16,0},... | collective-permute-start | bytes 491528 | tf_op jit(solution)/shard_map/ppermute | solution.py:271
  427.3 8.5 %collective-permute-start.33 = (bf16[4,64,896]{2,1,0:T(8,128)(2,1)S(1)}, bf16[4,64,896]{2,1,0:T(8,128)(2,1)S(1)}, u32[]{:S(2)}, u32[]{:S(2)}) collective-permute-start(bf16[4,64,896]{2,1,0:T(8,128)(2,1)S(1)} %fusion.84), channel_id=1, source_target_pairs={{0,4},{2,6},{4,0},{6,2},{8,12},{10,14},{12,8},{14,10},{16,20},{18,... | collective-permute-start | bytes 1376264 | tf_op jit(solution)/shard_map/ppermute | solution.py:266
  (58 other events, 509.7 us)
